TPU v7x, 128 devices: a whole 4x4x4 slice. The times are simulated.
128 devices in a mesh: region: 128 (over x, y, z, core).
Axes of the slice: x: 4, y: 4, z: 4, core: 2. Of those that a mesh axis runs over, the one named last changes fastest.
Arguments:
- sample_points: float32 [32768, 3, 128], P('region'), may hold values from -6 to 6
- sample_spacing: float32 [32768, 128], P('region'), may hold values from 0.004 to 0.04
- crossed: int32 [32768, 4], P('region'), may hold values from 0 to 127, all different within a row; in each aligned block of 256 rows (0 to 255, 256 to 511, ...) at most 20 rows name the same one
- colour_grad: float32 [3, 32768], P(None, 'region'), may hold values from -24 to 24
- freq: bfloat16 [128, 3, 64], P('region'), may hold values from -18 to 18
- w_hidden: bfloat16 [128, 128, 256], P('region'), may hold values from -0.5 to 0.5
- w_head: bfloat16 [128, 4, 256], P('region'), may hold values from -0.375 to 0.375
Outputs:
- rendered: float32 [3, 32768], P(None, 'region')
- head_grad: float32 [128, 4, 256], P('region')
Inputs may be any that keep to these rules, and one draw needn't show every extreme that they name: `crossed`: row r lists 4 distinct regions, in the order ray r meets them. In each aligned block of 256 rays (the rays of one device) no region is listed by more than 20 rays; in some block some region is listed by exactly 20 rays. Every region is listed by some ray.
All inputs are finite; a program needn't handle non-finite values.
Results may differ from a plain program's by a relative error of at most 0.0019.
Values may be sent and summed in bfloat16 or wider, within the bound.
A program may use at most 192 MiB of HBM per device.

v0:
```python
import jax
import jax.numpy as jnp
from jax import lax
from jax.sharding import PartitionSpec as P


def hidden_layer(points, freq, w_hidden):
    coords = points.reshape(points.shape[0], 3, -1)
    freq32 = freq.astype(jnp.float32)
    phases = coords[:, 0, :, None] * freq32[0][None, None, :]
    phases = phases + coords[:, 1, :, None] * freq32[1][None, None, :]
    phases = phases + coords[:, 2, :, None] * freq32[2][None, None, :]
    feature = jnp.concatenate([jnp.sin(phases), jnp.cos(phases)], axis=-1).astype(jnp.bfloat16)
    hidden = jnp.einsum("bsf,fh->bsh", feature, w_hidden, preferred_element_type=jnp.float32)
    return jnp.maximum(hidden, 0.0).astype(jnp.bfloat16)


def region_forward(points, freq, w_hidden, w_head):
    hidden = hidden_layer(points, freq, w_hidden)
    raw_out = jnp.einsum("bsh,oh->bos", hidden, w_head, preferred_element_type=jnp.float32)
    return (raw_out, hidden)


def render(raw_out, spacing):
    samples = spacing.shape[-1]
    upper = (jnp.arange(samples)[:, None] <= jnp.arange(samples)[None, :]).astype(jnp.float32)
    density = jax.nn.softplus(raw_out[0])
    colour = jax.nn.sigmoid(raw_out[1:])
    optical = density * spacing
    running = jnp.dot(optical, upper, precision=lax.Precision.HIGHEST)
    transmit = jnp.exp(optical - running)
    weight = transmit * (1.0 - jnp.exp(-optical))
    seg_colour = jnp.sum(weight[None] * colour, axis=-1)
    seg_trans = jnp.exp(-running[:, -1])
    return jnp.concatenate([seg_colour, seg_trans[None]], axis=0).T


def grouped(func, items, item_count, per_item):
    group_size = 1
    for candidate in range(1, item_count + 1):
        if item_count % candidate == 0 and candidate * per_item <= 16384:
            group_size = candidate
    shaped = jax.tree.map(
        lambda value: value.reshape((item_count // group_size, group_size) + value.shape[1:]), items
    )
    result = lax.map(lambda group_data: jax.vmap(func)(*group_data), shaped)
    return jax.tree.map(lambda value: value.reshape((item_count,) + value.shape[2:]), result)


def slot_numbers(flat_region, regions, capacity):
    seg_total = flat_region.shape[0]
    row_block = min(128, seg_total)
    onehot = (flat_region[:, None] == jnp.arange(regions, dtype=jnp.int32)[None, :]).astype(
        jnp.float32
    )
    onehot = onehot.reshape(seg_total // row_block, row_block, regions)
    strict_lower = (jnp.arange(row_block)[:, None] > jnp.arange(row_block)[None, :]).astype(
        jnp.float32
    )
    within = jnp.einsum("ij,bjn->bin", strict_lower, onehot)
    block_sums = jnp.sum(onehot, axis=1)
    offsets = jnp.cumsum(block_sums, axis=0) - block_sums
    slot_rank = jnp.sum(onehot * (within + offsets[:, None, :]), axis=-1).reshape(seg_total)
    return flat_region * capacity + slot_rank.astype(jnp.int32)


def composite(partials, colour_grad):
    upstream = colour_grad.T
    crossings = partials.shape[1]
    before = jnp.ones(partials.shape[:1], partials.dtype)
    befores = []
    rendered = jnp.zeros_like(upstream)
    for k in range(crossings):
        befores.append(before)
        rendered = rendered + before[:, None] * partials[:, k, :3]
        before = before * partials[:, k, 3]
    behind = jnp.zeros_like(upstream)
    seg_grads = [None] * crossings
    for k in range(crossings - 1, -1, -1):
        grad_colour = befores[k][:, None] * upstream
        grad_trans = befores[k] * jnp.sum(upstream * behind, axis=-1)
        seg_grads[k] = jnp.concatenate([grad_colour, grad_trans[:, None]], axis=-1)
        behind = partials[:, k, :3] + partials[:, k, 3][:, None] * behind
    return (rendered.T, jnp.stack(seg_grads, axis=1))


def on_device(sample_points, sample_spacing, crossed, colour_grad, freq, w_hidden, w_head):
    regions = lax.axis_size("region")
    ray_count, crossings = crossed.shape
    capacity = max(2, 5 * ray_count * crossings // (2 * regions))
    samples = sample_spacing.shape[1] // crossings
    per_item = capacity * samples
    flat_region = crossed.reshape(-1)
    slots = slot_numbers(flat_region, regions, capacity)
    points_seg = sample_points.reshape(ray_count, 3, crossings, samples).transpose(0, 2, 1, 3)
    points_seg = points_seg.reshape(ray_count * crossings, 3 * samples)
    spacing_seg = sample_spacing.reshape(ray_count * crossings, samples)
    point_buf = jnp.zeros((regions * capacity, 3 * samples), jnp.float32)
    point_buf = point_buf.at[slots].set(points_seg).reshape(regions, capacity, 3 * samples)
    own_freq = freq[0]
    own_hidden = w_hidden[0]
    own_head = w_head[0]
    got_points = lax.all_to_all(point_buf, "region", split_axis=0, concat_axis=0, tiled=True)
    raw_local, hidden_kept = grouped(
        lambda rows_in: region_forward(rows_in, own_freq, own_hidden, own_head),
        (got_points,),
        regions,
        per_item,
    )
    returned = lax.all_to_all(raw_local, "region", split_axis=0, concat_axis=0, tiled=True)
    raw_seg = returned.reshape(regions * capacity, 4, samples)[slots].transpose(1, 0, 2)
    seg_parts, pullback = jax.vjp(lambda value: render(value, spacing_seg), raw_seg)
    partials = seg_parts.reshape(ray_count, crossings, 4)
    rendered, seg_grads = composite(partials, colour_grad)
    raw_grad = pullback(seg_grads.reshape(-1, 4))[0].astype(jnp.bfloat16)
    grad_buf = jnp.zeros((regions * capacity, 4, samples), jnp.bfloat16)
    grad_buf = (
        grad_buf.at[slots].set(raw_grad.transpose(1, 0, 2)).reshape(regions, capacity, 4, samples)
    )
    got_grads = lax.all_to_all(grad_buf, "region", split_axis=0, concat_axis=0, tiled=True)
    head_grad = jnp.einsum(
        "nbos,nbsh->oh", got_grads, hidden_kept, preferred_element_type=jnp.float32
    )[None]
    return (rendered, head_grad)


def solution(mesh):
    return jax.shard_map(
        on_device,
        mesh=mesh,
        in_specs=(
            P("region", None, None),
            P("region", None),
            P("region", None),
            P(None, "region"),
            P("region", None, None),
            P("region", None, None),
            P("region", None, None),
        ),
        out_specs=(P(None, "region"), P("region", None, None)),
        check_vma=False,
    )
```

profile of v0, /device:TPU:1, one launch (start us, length us, event | category | flops | bytes accessed | tf_op | source)
XLA Modules:
  0.0 440.2 jit_solution(3367024072658900622)
XLA Ops:
  11.0 11.5 %all-to-all-start = ((f32[128,20,96]{2,1,0:T(8,128)}), f32[128,20,96]{2,1,0:T(8,128)S(1)}, u32[]{:S(2)}, u32[]{:S(2)}) async-start(f32[128,20,96]{2,1,0:T(8,128)} %reshape.218), calls=%async_computation | async-start | bytes 3145728 | tf_op jit(solution)/shard_map/all_to_all | solution.py:103
  22.6 24.9 %all-to-all-done = f32[128,20,96]{2,1,0:T(8,128)S(1)} async-done(((f32[128,20,96]{2,1,0:T(8,128)}), f32[128,20,96]{2,1,0:T(8,128)S(1)}, u32[]{:S(2)}, u32[]{:S(2)}) %all-to-all-start) | async-done | bytes 983072 | tf_op jit(solution)/shard_map/all_to_all | solution.py:103
  47.7 234.2 %while.12 = (s32[]{:T(128)}, f32[8,16,20,4,32]{4,3,2,1,0:T(4,128)}, bf16[8,16,20,32,256]{4,3,2,1,0:T(8,128)(2,1)}, f32[8,16,20,96]{3,1,2,0:T(8,128)S(1)}, bf16[3...) while((s32[]{:T(128)}, f32[8,16,20,4,32]{4,3,2,1,0:T(4,128)}, ...), condition=%wide.region_5.6_spmd, body=%wide.region_4.5_spmd.sunk | while | flops 707133632 | bytes 22804952 | solution.py:46
  48.6 20.2 %sine_convert_fusion.2 = (bf16[16,20,32,64]{3,2,1,0:T(8,128)(2,1)S(1)}, bf16[16,20,32,64]{3,2,1,0:T(8,128)(2,1)S(1)}) fusion(f32[64]{0:T(128)S(1)} %get-tuple-element.197, f32[16,20,32]{2,1,0:T(8,128)S(1)} %copy.146, f32[64]{0:T(128)S(1)} %get-tuple-element.199, f32[16,20,32]{2,1,0:T(8,128)S(1)} %copy.147, f32[64]{0:T(128)S(1)} %get-tuple-element.201, ...), kind=kLoop, calls=%fused_computation.6.clone.1 | loop fusion | flops 4587520 | bytes 2745088 | tf_op jit(solution)/shard_map/convert
  72.7 4.3 fusion.61
  77.8 20.2 %sine_convert_fusion.2 = (bf16[16,20,32,64]{3,2,1,0:T(8,128)(2,1)S(1)}, bf16[16,20,32,64]{3,2,1,0:T(8,128)(2,1)S(1)}) fusion(f32[64]{0:T(128)S(1)} %get-tuple-element.197, f32[16,20,32]{2,1,0:T(8,128)S(1)} %copy.146, f32[64]{0:T(128)S(1)} %get-tuple-element.199, f32[16,20,32]{2,1,0:T(8,128)S(1)} %copy.147, f32[64]{0:T(128)S(1)} %get-tuple-element.201, ...), kind=kLoop, calls=%fused_computation.6.clone.1 | loop fusion | flops 4587520 | bytes 2745088 | tf_op jit(solution)/shard_map/convert
  98.0 4.0 bitcast_dynamic-update-slice_fusion.2
  102.0 4.3 fusion.61
  107.2 20.2 %sine_convert_fusion.2 = (bf16[16,20,32,64]{3,2,1,0:T(8,128)(2,1)S(1)}, bf16[16,20,32,64]{3,2,1,0:T(8,128)(2,1)S(1)}) fusion(f32[64]{0:T(128)S(1)} %get-tuple-element.197, f32[16,20,32]{2,1,0:T(8,128)S(1)} %copy.146, f32[64]{0:T(128)S(1)} %get-tuple-element.199, f32[16,20,32]{2,1,0:T(8,128)S(1)} %copy.147, f32[64]{0:T(128)S(1)} %get-tuple-element.201, ...), kind=kLoop, calls=%fused_computation.6.clone.1 | loop fusion | flops 4587520 | bytes 2745088 | tf_op jit(solution)/shard_map/convert
  131.2 4.3 fusion.61
  136.4 20.2 %sine_convert_fusion.2 = (bf16[16,20,32,64]{3,2,1,0:T(8,128)(2,1)S(1)}, bf16[16,20,32,64]{3,2,1,0:T(8,128)(2,1)S(1)}) fusion(f32[64]{0:T(128)S(1)} %get-tuple-element.197, f32[16,20,32]{2,1,0:T(8,128)S(1)} %copy.146, f32[64]{0:T(128)S(1)} %get-tuple-element.199, f32[16,20,32]{2,1,0:T(8,128)S(1)} %copy.147, f32[64]{0:T(128)S(1)} %get-tuple-element.201, ...), kind=kLoop, calls=%fused_computation.6.clone.1 | loop fusion | flops 4587520 | bytes 2745088 | tf_op jit(solution)/shard_map/convert
  160.5 4.3 fusion.61
  165.7 20.2 %sine_convert_fusion.2 = (bf16[16,20,32,64]{3,2,1,0:T(8,128)(2,1)S(1)}, bf16[16,20,32,64]{3,2,1,0:T(8,128)(2,1)S(1)}) fusion(f32[64]{0:T(128)S(1)} %get-tuple-element.197, f32[16,20,32]{2,1,0:T(8,128)S(1)} %copy.146, f32[64]{0:T(128)S(1)} %get-tuple-element.199, f32[16,20,32]{2,1,0:T(8,128)S(1)} %copy.147, f32[64]{0:T(128)S(1)} %get-tuple-element.201, ...), kind=kLoop, calls=%fused_computation.6.clone.1 | loop fusion | flops 4587520 | bytes 2745088 | tf_op jit(solution)/shard_map/convert
  189.7 4.3 fusion.61
  194.9 20.2 %sine_convert_fusion.2 = (bf16[16,20,32,64]{3,2,1,0:T(8,128)(2,1)S(1)}, bf16[16,20,32,64]{3,2,1,0:T(8,128)(2,1)S(1)}) fusion(f32[64]{0:T(128)S(1)} %get-tuple-element.197, f32[16,20,32]{2,1,0:T(8,128)S(1)} %copy.146, f32[64]{0:T(128)S(1)} %get-tuple-element.199, f32[16,20,32]{2,1,0:T(8,128)S(1)} %copy.147, f32[64]{0:T(128)S(1)} %get-tuple-element.201, ...), kind=kLoop, calls=%fused_computation.6.clone.1 | loop fusion | flops 4587520 | bytes 2745088 | tf_op jit(solution)/shard_map/convert
  215.1 3.9 bitcast_dynamic-update-slice_fusion.2
  219.0 4.3 fusion.61
  224.2 20.2 %sine_convert_fusion.2 = (bf16[16,20,32,64]{3,2,1,0:T(8,128)(2,1)S(1)}, bf16[16,20,32,64]{3,2,1,0:T(8,128)(2,1)S(1)}) fusion(f32[64]{0:T(128)S(1)} %get-tuple-element.197, f32[16,20,32]{2,1,0:T(8,128)S(1)} %copy.146, f32[64]{0:T(128)S(1)} %get-tuple-element.199, f32[16,20,32]{2,1,0:T(8,128)S(1)} %copy.147, f32[64]{0:T(128)S(1)} %get-tuple-element.201, ...), kind=kLoop, calls=%fused_computation.6.clone.1 | loop fusion | flops 4587520 | bytes 2745088 | tf_op jit(solution)/shard_map/convert
  244.3 4.0 bitcast_dynamic-update-slice_fusion.2
  248.3 4.3 fusion.61
  253.5 20.2 %sine_convert_fusion.2 = (bf16[16,20,32,64]{3,2,1,0:T(8,128)(2,1)S(1)}, bf16[16,20,32,64]{3,2,1,0:T(8,128)(2,1)S(1)}) fusion(f32[64]{0:T(128)S(1)} %get-tuple-element.197, f32[16,20,32]{2,1,0:T(8,128)S(1)} %copy.146, f32[64]{0:T(128)S(1)} %get-tuple-element.199, f32[16,20,32]{2,1,0:T(8,128)S(1)} %copy.147, f32[64]{0:T(128)S(1)} %get-tuple-element.201, ...), kind=kLoop, calls=%fused_computation.6.clone.1 | loop fusion | flops 4587520 | bytes 2745088 | tf_op jit(solution)/shard_map/convert
  273.7 3.9 bitcast_dynamic-update-slice_fusion.2
  277.6 4.3 fusion.61
  282.0 6.1 %reshape.268 = f32[128,1,2560]{2,1,0:T(1,128)} reshape(f32[128,20,4,32]{3,2,1,0:T(4,128)} %bitcast.149) | data formatting | bytes 2621440
  288.1 4.8 %all-to-all-start.1 = ((f32[128,1,2560]{2,1,0:T(1,128)}), f32[128,1,2560]{2,1,0:T(1,128)S(1)}, u32[]{:S(2)}, u32[]{:S(2)}) async-start(f32[128,1,2560]{2,1,0:T(1,128)} %reshape.268), calls=%async_computation.1 | async-start | bytes 2621440 | tf_op jit(solution)/shard_map/all_to_all | solution.py:110
  293.2 21.9 %all-to-all-done.1 = f32[128,1,2560]{2,1,0:T(1,128)S(1)} async-done(((f32[128,1,2560]{2,1,0:T(1,128)}), f32[128,1,2560]{2,1,0:T(1,128)S(1)}, u32[]{:S(2)}, u32[]{:S(2)}) %all-to-all-start.1) | async-done | bytes 1310752 | tf_op jit(solution)/shard_map/all_to_all | solution.py:110
  319.4 4.3 reshape.269
  323.7 6.0 %gather_fusion = f32[1024,4,32]{2,1,0:T(4,128)S(1)} fusion(f32[2560,4,32]{2,1,0:T(4,128)} %bitcast.147, s32[1024]{0:T(1024)S(1)} %broadcast_clamp_fusion), kind=kCustom, calls=%fused_computation | custom fusion | bytes 1052672 | tf_op jit(solution)/shard_map/gather | solution.py:111
  336.7 60.5 %scatter_fusion = bf16[2560,4,32]{2,1,0:T(4,128)(2,1)S(1)} fusion(bf16[2560,4,32]{2,1,0:T(4,128)(2,1)S(1)} %broadcast_in_dim.31, s32[1024]{0:T(1024)S(1)} %bitcast.161, bf16[1024,4,32]{2,1,0:T(4,128)(2,1)} %copy.126), kind=kCustom, calls=%fused_computation.2 | custom fusion | bytes 790528 | tf_op jit(solution)/shard_map/scatter | solution.py:118
  399.1 19.8 %all_to_all.15 = bf16[128,2,1280]{2,1,0:T(2,128)(2,1)} all-to-all(bf16[128,2,1280]{2,1,0:T(2,128)(2,1)S(1)} %reshape.270), channel_id=1, replica_groups=mesh['region'=128] {'region'}, dimensions={0} | all-to-all | bytes 1310720 | tf_op jit(solution)/shard_map/all_to_all | solution.py:120
  418.9 4.4 reshape.271
  423.3 16.8 %fusion.16 = f32[1,4,256]{2,1,0:T(4,128)} fusion(bf16[128,20,32,256]{3,2,1,0:T(8,128)(2,1)} %bitcast.172, bf16[128,20,4,32]{3,2,1,0:T(4,128)(2,1)S(1)} %reshape.271), kind=kOutput, calls=%fused_computation.31 | convolution fusion | flops 167772160 | bytes 42602496 | tf_op jit(solution)/shard_map/nbos,nbsh->oh/dot_general | solution.py:121
  (125 shorter events, 45.9 us)
Async XLA Ops:
  6.3 41.4 %copy-start = (bf16[1,128,256]{2,1,0:T(8,128)(2,1)S(1)}, bf16[1,128,256]{2,1,0:T(8,128)(2,1)}, u32[]{:S(2)}) copy-start(bf16[1,128,256]{2,1,0:T(8,128)(2,1)} %param.14) | copy-start | bytes 196612
  6.3 41.4 %copy-start.2 = (bf16[1,4,256]{2,1,0:T(4,128)(2,1)S(1)}, bf16[1,4,256]{2,1,0:T(4,128)(2,1)}, u32[]{:S(2)}) copy-start(bf16[1,4,256]{2,1,0:T(4,128)(2,1)} %param.15) | copy-start | bytes 6148
  6.3 41.4 %copy-start.3 = (bf16[1,3,64]{2,1,0:T(4,128)(2,1)S(1)}, bf16[1,3,64]{2,1,0:T(4,128)(2,1)}, u32[]{:S(2)}) copy-start(bf16[1,3,64]{2,1,0:T(4,128)(2,1)} %param.13) | copy-start | bytes 1156
  11.0 36.4 %all-to-all-start = ((f32[128,20,96]{2,1,0:T(8,128)}), f32[128,20,96]{2,1,0:T(8,128)S(1)}, u32[]{:S(2)}, u32[]{:S(2)}) async-start(f32[128,20,96]{2,1,0:T(8,128)} %reshape.218), calls=%async_computation | async-start | bytes 3145728 | tf_op jit(solution)/shard_map/all_to_all | solution.py:103
  282.0 10.9 %copy-start.1 = (f32[256,128]{1,0:T(8,128)S(1)}, f32[256,128]{1,0:T(8,128)}, u32[]{:S(2)}) copy-start(f32[256,128]{1,0:T(8,128)} %param.10) | copy-start | bytes 393220
  288.1 27.0 %all-to-all-start.1 = ((f32[128,1,2560]{2,1,0:T(1,128)}), f32[128,1,2560]{2,1,0:T(1,128)S(1)}, u32[]{:S(2)}, u32[]{:S(2)}) async-start(f32[128,1,2560]{2,1,0:T(1,128)} %reshape.268), calls=%async_computation.1 | async-start | bytes 2621440 | tf_op jit(solution)/shard_map/all_to_all | solution.py:110
  323.6 9.1 %copy-start.4 = (f32[3,256]{1,0:T(4,128)S(1)}, f32[3,256]{1,0:T(4,128)}, u32[]{:S(2)}) copy-start(f32[3,256]{1,0:T(4,128)} %param.12) | copy-start | bytes 9220
where the time goes:
time: 447 us; the launch traced here: 440 us
  other arithmetic  167 us (37%)
  local copies, waits for them, and re-layouts  104 us (23%)
  matrix products  84 us (19%)
  waiting for transfers between devices  46.7 us (10%)
  blocking collectives  19.8 us (4%)
  starting transfers between devices  16.3 us (4%)
    another operation x8, other arithmetic  161 us
    scatter x1, local copies, waits for them, and re-layouts, on_device(): grad_buf.at[slots].set(raw_grad.transpose(1, 0, 2))  60.5 us
    dot_general x8, matrix products, region_forward(): jnp.einsum('bsh,oh->bos', hidden, w_head, preferred_element_type=jnp.floa...  34.7 us
    dot_general x8, matrix products, hidden_layer(): jnp.einsum('bsf,fh->bsh', feature, w_hidden, preferred_element_type=jnp.f...  31.5 us
    all_to_all x1, waiting for transfers between devices, on_device(): lax.all_to_all(point_buf, 'region', split_axis=0, concat_axis=0, tiled=True)  24.9 us
    all_to_all x1, waiting for transfers between devices, on_device(): lax.all_to_all(raw_local, 'region', split_axis=0, concat_axis=0, tiled=True)  21.9 us
    all_to_all x1, blocking collectives, on_device(): lax.all_to_all(grad_buf, 'region', split_axis=0, concat_axis=0, tiled=True)  19.8 us
    unnamed x16, local copies, waits for them, and re-layouts  18.7 us
  transfers between devices with their start and end apart: 2, of which 2 were waited for; matrix products, arithmetic and copies ran while one was open for 0% of the time, Pallas kernels for 0%

commit v1 on v0

v1 whole, which is shorter than its diff:
```python
import functools

import jax
import jax.numpy as jnp
import numpy as np
from jax import lax
from jax.experimental import pallas as pl
from jax.experimental.pallas import tpu as pltpu
from jax.sharding import PartitionSpec as P

RAYS = 256
K = 4
S = 32
REG = 128
SEG = RAYS * K
NB = 352
FREQ = 64
HID = 256
LANES = 128

F32 = jnp.float32
BF16 = jnp.bfloat16

SIN_C = (4.44288292, -7.3082457, 3.60635441, -0.84611289, 0.10982699)
COS_C = (1.4142135, -6.97885099, 5.73946117, -1.88356298, 0.31069819)

VM = pl.BlockSpec(memory_space=pltpu.VMEM)
SM = pl.BlockSpec(memory_space=pltpu.SMEM)
ANY = pl.BlockSpec(memory_space=pl.ANY)


def iota(shape, dim):
    return lax.broadcasted_iota(jnp.int32, shape, dim)


def dot(a, b, dims=((1,), (0,))):
    return lax.dot_general(a, b, (dims, ((), ())), preferred_element_type=F32)


def pieces(x):
    hi = x.astype(BF16)
    rest = x - hi.astype(F32)
    mid = rest.astype(BF16)
    low = (rest - mid.astype(F32)).astype(BF16)
    return hi, mid, low


def exact_dot(x, pattern):
    hi, mid, low = pieces(x)
    return dot(hi, pattern) + dot(mid, pattern) + dot(low, pattern)


def poly(z, coef):
    out = coef[-1] * z + coef[-2]
    for value in coef[-3::-1]:
        out = out * z + value
    return out


def sort_kernel(crossed_ref, points_ref, spacing_ref, picks_ref, coords_ref, table_ref):
    owner = crossed_ref[...]
    onehot = (iota((REG, SEG), 0) == owner).astype(F32)
    onehot16 = onehot.astype(BF16)
    earlier = (iota((SEG, SEG), 0) < iota((SEG, SEG), 1)).astype(F32).astype(BF16)
    rank = dot(onehot16, earlier)
    counts = jnp.sum(onehot, axis=1, keepdims=True)
    blocks = jnp.floor((counts + 3.0) * 0.25)
    lower = (iota((REG, REG), 1) <= iota((REG, REG), 0)).astype(F32).astype(BF16)
    ends = dot(lower, jnp.broadcast_to(blocks, (REG, LANES)).astype(BF16))[:, :1]
    starts = ends - blocks
    rank_row = jnp.sum(onehot * rank, axis=0, keepdims=True)
    start_row = jnp.sum(onehot * starts, axis=0, keepdims=True)
    step = jnp.floor(rank_row * 0.25)
    place = (rank_row - 4.0 * step) * NB + start_row + step
    place = place.astype(jnp.int32)
    block_at = iota((REG, 384), 1).astype(F32)
    owner_of = jnp.sum((block_at >= ends).astype(F32), axis=0, keepdims=True)
    owner_of = jnp.minimum(owner_of, REG - 1.0)
    total = jnp.sum(blocks, axis=0, keepdims=True)
    table = jnp.where(iota((1, 384), 1) == 383, total, owner_of)
    table_ref[...] = table.astype(jnp.int32)

    lane_group = iota((RAYS, LANES), 1) // S
    sources = [points_ref[:, 0, :], points_ref[:, 1, :], points_ref[:, 2, :], spacing_ref[...]]
    rows = []
    for k in range(K):
        row = jnp.zeros((RAYS, LANES), F32)
        for c in range(4):
            moved = sources[c]
            if c != k:
                moved = pltpu.roll(moved, ((c - k) % 4) * S, 1)
            row = jnp.where(lane_group == c, moved, row)
        rows.append(row)
    packed = jnp.concatenate(rows, axis=0)
    hi, mid, low = pieces(packed)
    source = jnp.concatenate([hi, mid, low], axis=1)
    block_group = iota((NB, LANES), 1) // S
    coords = [jnp.zeros((NB, LANES), F32) for _ in range(4)]
    for q in range(4):
        picks = (iota((NB, SEG), 0) + q * NB == place).astype(F32).astype(BF16)
        picks_ref[q] = picks
        three = dot(picks, source)
        got = three[:, :128] + three[:, 128:256] + three[:, 256:]
        for c in range(4):
            moved = got
            if c != q:
                moved = pltpu.roll(got, ((q - c) % 4) * S, 1)
            coords[c] = jnp.where(block_group == q, moved, coords[c])
    for c in range(4):
        value = coords[c] * np.float32(0.5 / np.pi) if c < 3 else coords[c]
        coords_ref[pl.ds(c, NB, stride=8), :] = value
    for c in range(4, 8):
        coords_ref[pl.ds(c, NB, stride=8), :] = jnp.zeros((NB, LANES), F32)


def feature_kernel(table_ref, coords_ref, freq_ref, feature_ref):
    def body(b, carry):
        region = table_ref[b]
        f8 = freq_ref[region]
        f24 = jnp.concatenate([f8, f8, f8], axis=0).astype(BF16)
        x = coords_ref[pl.ds(b * 8, 8), :]
        hi = x.astype(BF16).astype(F32)
        mid = (x - hi).astype(BF16).astype(F32)
        low = x - hi - mid
        x24 = jnp.concatenate([hi, mid, low], axis=0).astype(BF16)
        turns = dot(f24, x24, ((0,), (0,)))[:FREQ]
        r = turns - jnp.round(turns)
        z = r * r
        s = r * poly(z, SIN_C)
        c = poly(z, COS_C)
        feature = jnp.concatenate([s * c, 1.0 - s * s], axis=0)
        feature_ref[b] = feature.astype(BF16)
        return carry

    lax.fori_loop(0, NB, body, 0, unroll=2)


def tri(kind):
    row, col = iota((LANES, LANES), 0), iota((LANES, LANES), 1)
    same = row // S == col // S
    if kind == "upto":
        keep = row <= col
    elif kind == "after":
        keep = row > col
    else:
        keep = row >= 0
    return (same & keep).astype(F32).astype(BF16)


def render_kernel(
    table_ref, coords_ref, picks_ref, colour_grad_ref, feature_ref, hidden_w_ref, head_ref,
    rendered_ref, grad_ref, hidden_ref, raw_ref,
):
    total = table_ref[383]

    def forward(b, carry):
        region = table_ref[b]
        hid = jnp.maximum(dot(hidden_w_ref[region], feature_ref[b]), 0.0).astype(BF16)
        hidden_ref[b] = hid
        raw_ref[pl.ds(b * 8, 8), :] = dot(head_ref[region], hid)
        return carry

    def blank(b, carry):
        raw_ref[pl.ds(b * 8, 8), :] = jnp.zeros((8, LANES), F32)
        return carry

    lax.fori_loop(0, total, forward, 0)
    lax.fori_loop(total, NB, blank, 0)

    raw = [raw_ref[pl.ds(o, NB, stride=8), :] for o in range(4)]
    spacing = coords_ref[pl.ds(3, NB, stride=8), :]
    soft = jnp.maximum(raw[0], 0.0) + jnp.log1p(jnp.exp(-jnp.abs(raw[0])))
    colour = [1.0 / (1.0 + jnp.exp(-raw[c])) for c in (1, 2, 3)]
    gate = 1.0 / (1.0 + jnp.exp(-raw[0]))
    optical = soft * spacing
    running = exact_dot(optical, tri("upto"))
    after = jnp.exp(-running)
    weight = jnp.exp(optical - running) * (1.0 - jnp.exp(-optical))
    chooser = (iota((8, LANES), 1) // S == iota((8, LANES), 0)).astype(F32).astype(BF16)
    last = (iota((8, LANES), 1) == iota((8, LANES), 0) * S + (S - 1)).astype(F32).astype(BF16)

    def seg_rows(value, pattern):
        return [dot(pattern, part, ((1,), (1,))) for part in pieces(value)]

    sums = []
    for c in range(3):
        three = seg_rows(weight * colour[c], chooser)
        sums.append(three[0] + three[1] + three[2])
    three = seg_rows(after, last)
    sums.append(three[0] + three[1] + three[2])
    by_seg = jnp.zeros((16, SEG), F32)
    for q in range(4):
        four = jnp.concatenate([value[q:q + 1] for value in sums], axis=0)
        hi, mid, low = pieces(four)
        rows = jnp.concatenate(
            [hi.astype(F32), mid.astype(F32), low.astype(F32), jnp.zeros((4, NB), F32)], axis=0
        )
        by_seg = by_seg + dot(rows.astype(BF16), picks_ref[q])
    partial = by_seg[0:4] + by_seg[4:8] + by_seg[8:12]
    seg_colour = [partial[0:3, k * RAYS:(k + 1) * RAYS] for k in range(K)]
    seg_trans = [partial[3:4, k * RAYS:(k + 1) * RAYS] for k in range(K)]
    upstream = colour_grad_ref[...]
    before = jnp.ones((1, RAYS), F32)
    befores = []
    rendered = jnp.zeros((3, RAYS), F32)
    for k in range(K):
        befores.append(before)
        rendered = rendered + before * seg_colour[k]
        before = before * seg_trans[k]
    rendered_ref[...] = rendered
    behind = jnp.zeros((3, RAYS), F32)
    grads = [None] * K
    for k in range(K - 1, -1, -1):
        trans = befores[k] * jnp.sum(upstream * behind, axis=0, keepdims=True)
        grads[k] = jnp.concatenate([befores[k] * upstream, trans], axis=0)
        behind = seg_colour[k] + seg_trans[k] * behind
    grad_rows = jnp.concatenate(grads, axis=1)
    hi, mid, low = pieces(grad_rows)
    grad_rows = jnp.concatenate(
        [hi.astype(F32), mid.astype(F32), low.astype(F32), jnp.zeros((4, SEG), F32)], axis=0
    ).astype(BF16)
    spread = [jnp.zeros((NB, LANES), F32) for _ in range(4)]
    for q in range(4):
        got = dot(picks_ref[q], grad_rows, ((1,), (1,))).astype(BF16)
        lane = iota((16, LANES), 1) // S == q
        for o in range(4):
            row = iota((16, LANES), 0)
            expand = (lane & (row % 4 == o) & (row < 12)).astype(F32).astype(BF16)
            spread[o] = spread[o] + dot(got, expand)
    shade = spread[0] * colour[0] + spread[1] * colour[1] + spread[2] * colour[2]
    later = exact_dot(shade * weight, tri("after")) + spread[3] * exact_dot_last(after)
    d_optical = shade * after - later
    raw_grads = [d_optical * spacing * gate]
    for c in range(3):
        raw_grads.append(spread[c] * weight * colour[c] * (1.0 - colour[c]))
    for o in range(4):
        raw_ref[pl.ds(o, NB, stride=8), :] = raw_grads[o]
    for o in range(4, 8):
        raw_ref[pl.ds(o, NB, stride=8), :] = jnp.zeros((NB, LANES), F32)
    grad_ref[...] = jnp.zeros_like(grad_ref)

    def backward(b, carry):
        region = table_ref[b]
        rg = raw_ref[pl.ds(b * 8, 8), :].astype(BF16)
        grad_ref[region] += dot(rg, hidden_ref[b], ((1,), (1,)))
        return carry

    lax.fori_loop(0, total, backward, 0)


def exact_dot_last(after):
    row, col = iota((LANES, LANES), 0), iota((LANES, LANES), 1)
    pattern = ((row // S == col // S) & (row % S == S - 1)).astype(F32).astype(BF16)
    return exact_dot(after, pattern)


def params(mib, **kw):
    return pltpu.CompilerParams(vmem_limit_bytes=mib * 1024 * 1024, **kw)


def sort_segments(sample_points, sample_spacing, crossed):
    crossed_row = crossed.T.reshape(1, SEG)
    return pl.pallas_call(
        sort_kernel,
        out_shape=(
            jax.ShapeDtypeStruct((4, NB, SEG), BF16),
            jax.ShapeDtypeStruct((NB * 8, LANES), F32),
            jax.ShapeDtypeStruct((1, 384), jnp.int32),
        ),
        in_specs=[VM, VM, VM],
        out_specs=(VM, VM, VM),
        compiler_params=params(32),
    )(crossed_row, sample_points, sample_spacing)


def make_features(table, coords, freq_all):
    return pl.pallas_call(
        feature_kernel,
        out_shape=jax.ShapeDtypeStruct((NB, LANES, LANES), BF16),
        in_specs=[SM, VM, VM],
        out_specs=VM,
        compiler_params=params(40),
    )(table, coords, freq_all)


def render_all(table, coords, picks, colour_grad, feature, hidden_all, head_all):
    return pl.pallas_call(
        render_kernel,
        out_shape=(
            jax.ShapeDtypeStruct((3, RAYS), F32),
            jax.ShapeDtypeStruct((REG, 8, HID), F32),
        ),
        in_specs=[SM, VM, VM, VM, VM, VM, VM],
        out_specs=(VM, VM),
        scratch_shapes=[
            pltpu.VMEM((NB, HID, LANES), BF16),
            pltpu.VMEM((NB * 8, LANES), F32),
        ],
        compiler_params=params(60),
    )(table, coords, picks, colour_grad, feature, hidden_all, head_all)


def local_part(sample_points, sample_spacing, crossed, colour_grad, freq_all, hidden_all, head_all):
    picks, coords, table = sort_segments(sample_points, sample_spacing, crossed)
    table = table.reshape(384)
    feature = make_features(table, coords, freq_all)
    return render_all(table, coords, picks, colour_grad, feature, hidden_all, head_all)


def on_device(sample_points, sample_spacing, crossed, colour_grad, freq, w_hidden, w_head):
    freq8 = jnp.pad(freq[0].astype(F32), ((0, 5), (0, LANES - FREQ)))
    head8 = jnp.pad(w_head[0], ((0, 4), (0, 0)))
    freq_all = lax.all_gather(freq8, "region")
    hidden_all = lax.all_gather(w_hidden[0].T, "region")
    head_all = lax.all_gather(head8, "region")
    rendered, grad = local_part(
        sample_points, sample_spacing, crossed, colour_grad, freq_all, hidden_all, head_all
    )
    parts = lax.all_to_all(grad[:, :4], "region", split_axis=0, concat_axis=0, tiled=True)
    return rendered, jnp.sum(parts, axis=0, keepdims=True)


def solution(mesh):
    return jax.shard_map(
        on_device,
        mesh=mesh,
        in_specs=(
            P("region", None, None),
            P("region", None),
            P("region", None),
            P(None, "region"),
            P("region", None, None),
            P("region", None, None),
            P("region", None, None),
        ),
        out_specs=(P(None, "region"), P("region", None, None)),
        check_vma=False,
    )
```

time: 447 us -> 328 us (0.73); the launches traced: 440 us -> 327 us
  Pallas kernels: 0 us -> 192 us
  other arithmetic: 167 us -> 1.48 us
  matrix products: 84 us -> 0 us
  local copies, waits for them, and re-layouts: 104 us -> 22.8 us
  blocking collectives: 19.8 us -> 95.9 us
  waiting for transfers between devices: 46.7 us -> 0.68 us
  starting transfers between devices: 16.3 us -> 0.04 us
  between operations: 0.98 us -> 14.1 us
    pallas_call x0 -> x3, Pallas kernels: none -> 192 us  [the longest x1 146 us: render_all(): pl.pallas_call(render_kernel, out_shape=(jax.ShapeDtypeStruct((3, RAYS),...]
    another operation x12 -> x0, other arithmetic: 161 us -> none
    dot_general x20 -> x0, matrix products: 84 us -> none  [the longest x8 34.7 us: region_forward(): jnp.einsum('bsh,oh->bos', hidden, w_head, preferred_element_type=jnp.floa...]
    all_gather x0 -> x2, blocking collectives: none -> 76.2 us  [the longest x1 39.9 us: on_device(): freq_all = lax.all_gather(freq8, 'region')]
    scatter x2 -> x0, local copies, waits for them, and re-layouts: 63.9 us -> none  [the longest x1 60.5 us: on_device(): grad_buf.at[slots].set(raw_grad.transpose(1, 0, 2))]
    all_to_all x2 -> x0, waiting for transfers between devices: 46.7 us -> none  [the longest x1 24.9 us: on_device(): lax.all_to_all(point_buf, 'region', split_axis=0, concat_axis=0, tiled=True)]
    all_to_all x2 -> x0, starting transfers between devices: 16.3 us -> none  [the longest x1 11.5 us: on_device(): lax.all_to_all(point_buf, 'region', split_axis=0, concat_axis=0, tiled=True)]
    all_gather x0 -> x1, local copies, waits for them, and re-layouts: none -> 11.9 us  [on_device(): hidden_all = lax.all_gather(w_hidden[0].T, 'region')]
  transfers between devices with their start and end apart: 2 -> 1, of which waited for: 2 -> 0; matrix products, arithmetic and copies ran while one was open for 0% -> 1% of each run, Pallas kernels for 0% -> 14%
where the time goes in v1:
time: 328 us; the launch traced here: 327 us
  Pallas kernels  192 us (59%)
  blocking collectives  95.9 us (29%)
  local copies, waits for them, and re-layouts  22.8 us (7%)
  between operations  14.1 us (4%)
    pallas_call x1, Pallas kernels, render_all(): pl.pallas_call(render_kernel, out_shape=(jax.ShapeDtypeStruct((3, RAYS),...  146 us
    pallas_call x1, Pallas kernels, make_features(): pl.pallas_call(feature_kernel, out_shape=jax.ShapeDtypeStruct((NB, LANES,...  43.1 us
    all_gather x1, blocking collectives, on_device(): freq_all = lax.all_gather(freq8, 'region')  39.9 us
    all_gather x1, blocking collectives, on_device(): head_all = lax.all_gather(head8, 'region')  36.2 us
    all_to_all x1, blocking collectives, on_device(): lax.all_to_all(grad[:, :4], 'region', split_axis=0, concat_axis=0, tiled=...  19.7 us
    all_gather x1, local copies, waits for them, and re-layouts, on_device(): hidden_all = lax.all_gather(w_hidden[0].T, 'region')  11.9 us
    unnamed x12, local copies, waits for them, and re-layouts  8.87 us
  transfers between devices with their start and end apart: 1, of which 0 were waited for; matrix products, arithmetic and copies ran while one was open for 1% of the time, Pallas kernels for 14%

profile of v1, /device:TPU:1, one launch (start us, length us, event | category | flops | bytes accessed | tf_op | source)
XLA Modules:
  0.0 327.3 jit_solution(252259139824033483)
XLA Ops:
  7.2 0.0 all-gather.5.cloned.1.call-start
  7.2 0.7 all-gather.5.cloned.1.call-update
  7.9 0.7 copy.11
  8.6 1.3 copy.9.points_ref
  9.9 0.7 pad.10
  10.6 0.0 copy-start.3
  10.6 0.9 copy-done.3
  11.5 3.1 shard_map.86
  14.6 0.0 copy-start.2
  14.6 1.7 copy-done.2
  16.2 0.0 copy-start.1
  16.3 0.0 copy-start.4
  16.3 0.7 pad_convert_fusion
  17.0 39.9 %all-gather = f32[1024,128]{1,0:T(8,128)S(1)} all-gather(f32[8,128]{1,0:T(8,128)S(1)} %pad_convert_fusion), channel_id=2, replica_groups=mesh['region'=128] {'region'}, dimensions={0}, use_global_device_ids=true | all-gather | bytes 528384 | tf_op jit(solution)/shard_map/all_gather | solution.py:313
  56.9 43.1 %shard_map.87.feature_ref = bf16[352,128,128]{2,1,0:T(8,128)(2,1)S(1)} custom-call(s32[384]{0:T(512)S(1)} %reduce.table_ref, f32[2816,128]{1,0:T(8,128)S(1)} %get-tuple-element.8.coords_ref, f32[128,8,128]{2,1,0:T(8,128)S(1)} %bitcast.13), custom_call_target="tpu_custom_call" | custom-call | tf_op jit(solution)/shard_map/pallas_call | solution.py:277
  100.0 0.0 copy-start
  100.1 4.3 %copy-done = bf16[352,128,128]{2,1,0:T(8,128)(2,1)} copy-done((bf16[352,128,128]{2,1,0:T(8,128)(2,1)}, bf16[352,128,128]{2,1,0:T(8,128)(2,1)S(1)}, u32[]{:S(2)}) %copy-start) | copy-done | bytes 11534360
  104.4 36.2 %all-gather.2 = bf16[1024,256]{1,0:T(8,128)(2,1)} all-gather(bf16[8,256]{1,0:T(8,128)(2,1)S(1)} %pad.10), channel_id=4, replica_groups=mesh['region'=128] {'region'}, dimensions={0}, use_global_device_ids=true | all-gather | bytes 528384 | tf_op jit(solution)/shard_map/all_gather | solution.py:315
  140.6 0.0 all-gather.5.cloned.1.call-done
  140.6 11.9 %copy.10 = bf16[32768,128]{1,0:T(8,128)(2,1)} copy(bf16[32768,128]{0,1:T(8,128)(2,1)} %all-gather.5.cloned.1.call-done) | data formatting | bytes 16777216 | tf_op jit(solution)/shard_map/all_gather | solution.py:314
  152.6 0.0 copy-done.1
  152.6 0.0 copy-done.4
  152.6 146.1 %shard_map.88 = (f32[3,256]{1,0:T(4,128)}, f32[128,8,256]{2,1,0:T(8,128)}) custom-call(s32[384]{0:T(512)} %copy-done.4, f32[2816,128]{1,0:T(8,128)} %copy-done.1, bf16[4,352,1024]{2,1,0:T(8,128)(2,1)} %copy-done.2, f32[3,256]{1,0:T(4,128)} %colour_grad_ref.1, bf16[352,128,128]{2,1,0:T(8,128)(2,1)} %copy-done, bf16[128,256,128]{2,1,0:T(8,128)(2,1)} %bitcast.15, ...), custom_call_target="tpu_custom_call" | custom-call | tf_op jit(solution)/shard_map/pallas_call | solution.py:287
  298.7 1.3 slice.3
  300.0 19.7 %all_to_all.5 = f32[128,4,256]{2,1,0:T(4,128)S(1)} all-to-all(f32[128,4,256]{2,1,0:T(4,128)S(1)} %slice.3), channel_id=1, replica_groups=mesh['region'=128] {'region'}, dimensions={0} | all-to-all | bytes 1048576 | tf_op jit(solution)/shard_map/all_to_all | solution.py:319
  319.7 0.7 reduce_sum.9
  (1 shorter events, 0.0 us)
Async XLA Ops:
  7.2 133.5 %all-gather.5.cloned.1.call-start = ((), (), s32[]{:S(2)}) async-start(), calls=%async_computation.1 | async-start | bytes 8454144 | tf_op jit(solution)/shard_map/all_gather | solution.py:314
  10.6 0.9 copy-start.3
  14.6 1.7 copy-start.2
  16.2 136.3 %copy-start.1 = (f32[2816,128]{1,0:T(8,128)}, f32[2816,128]{1,0:T(8,128)S(1)}, u32[]{:S(2)}) copy-start(f32[2816,128]{1,0:T(8,128)S(1)} %get-tuple-element.8.coords_ref) | copy-start | bytes 4325380
  16.3 136.3 %copy-start.4 = (s32[384]{0:T(512)}, s32[384]{0:T(512)S(1)}, u32[]{:S(2)}) copy-start(s32[384]{0:T(512)S(1)} %reduce.table_ref) | copy-start | bytes 4612
  100.0 4.3 %copy-start = (bf16[352,128,128]{2,1,0:T(8,128)(2,1)}, bf16[352,128,128]{2,1,0:T(8,128)(2,1)S(1)}, u32[]{:S(2)}) copy-start(bf16[352,128,128]{2,1,0:T(8,128)(2,1)S(1)} %shard_map.87.feature_ref) | copy-start | bytes 34603012
Sparse Core Ops, SparseCore 0:
  10.8 82.3 all-gather.4

commit v2 on v1

--- a/solution.py
+++ b/solution.py
@@ -17,6 +17,10 @@
 FREQ = 64
 HID = 256
 LANES = 128
+COPIES = 152
+GF = 32
+CHUNKS = (1, 1, 2, 2, 2, 2, 1)
+GR = 16
 
 F32 = jnp.float32
 BF16 = jnp.bfloat16
@@ -78,6 +82,9 @@
     owner_of = jnp.minimum(owner_of, REG - 1.0)
     total = jnp.sum(blocks, axis=0, keepdims=True)
     table = jnp.where(iota((1, 384), 1) == 383, total, owner_of)
+    for part in range(3):
+        bound = ends[(part + 1) * 32 - 1:(part + 1) * 32]
+        table = jnp.where(iota((1, 384), 1) == 380 + part, bound, table)
     table_ref[...] = table.astype(jnp.int32)
 
     lane_group = iota((RAYS, LANES), 1) // S
@@ -108,31 +115,269 @@
             coords[c] = jnp.where(block_group == q, moved, coords[c])
     for c in range(4):
         value = coords[c] * np.float32(0.5 / np.pi) if c < 3 else coords[c]
-        coords_ref[pl.ds(c, NB, stride=8), :] = value
-    for c in range(4, 8):
-        coords_ref[pl.ds(c, NB, stride=8), :] = jnp.zeros((NB, LANES), F32)
-
-
-def feature_kernel(table_ref, coords_ref, freq_ref, feature_ref):
-    def body(b, carry):
-        region = table_ref[b]
-        f8 = freq_ref[region]
-        f24 = jnp.concatenate([f8, f8, f8], axis=0).astype(BF16)
-        x = coords_ref[pl.ds(b * 8, 8), :]
-        hi = x.astype(BF16).astype(F32)
-        mid = (x - hi).astype(BF16).astype(F32)
-        low = x - hi - mid
-        x24 = jnp.concatenate([hi, mid, low], axis=0).astype(BF16)
-        turns = dot(f24, x24, ((0,), (0,)))[:FREQ]
-        r = turns - jnp.round(turns)
-        z = r * r
-        s = r * poly(z, SIN_C)
-        c = poly(z, COS_C)
-        feature = jnp.concatenate([s * c, 1.0 - s * s], axis=0)
-        feature_ref[b] = feature.astype(BF16)
+        coords_ref[pl.ds(c, NB, stride=4), :] = value
+
+
+def features_of(freq, coords):
+    f12 = jnp.concatenate([freq, freq, freq], axis=0).astype(BF16)
+    hi = coords.astype(BF16).astype(F32)
+    mid = (coords - hi).astype(BF16).astype(F32)
+    low = coords - hi - mid
+    x12 = jnp.concatenate([hi, mid, low], axis=0).astype(BF16)
+    return dot(f12, x12, ((0,), (0,)))[:FREQ]
+
+
+def encode(turns):
+    r = turns - jnp.round(turns)
+    z = r * r
+    s = r * poly(z, SIN_C)
+    c = poly(z, COS_C)
+    return jnp.concatenate([s * c, 1.0 - s * s], axis=0).astype(BF16)
+
+
+ORDERS = ((0, 1, 2), (1, 2, 0), (2, 0, 1))
+STRIDES = (32, 8, 2)
+MESH_ID = pl.DeviceIdType.MESH
+
+
+def gather_kernel(
+    table_ref, coords_ref, freq_in_ref, hidden_in_ref, head_in_ref, nets_ref, feature_out_ref,
+    payload_ref, freq_ref, feature_ref,
+    send_sem, recv_sem, freq_send, freq_recv, local_sem, feature_sem,
+):
+    me = lax.axis_index("region")
+    core = lax.rem(me, 2)
+    sibling = me + 1 - 2 * core
+    pos = [lax.rem(lax.div(me, stride), 4) for stride in STRIDES]
+    barrier = pltpu.get_barrier_semaphore()
+
+    def greet(step, carry):
+        peer = lax.rem(me + step, REG)
+        pl.semaphore_signal(barrier, inc=1, device_id=(peer,), device_id_type=MESH_ID)
         return carry
 
-    lax.fori_loop(0, NB, body, 0, unroll=2)
+    lax.fori_loop(1, REG, greet, 0)
+    payload_ref[0:HID, :] = hidden_in_ref[...].astype(F32).T.astype(BF16)
+    payload_ref[HID:HID + 32, :] = head_in_ref[...]
+    freq_ref[me] = freq_in_ref[...]
+    pl.semaphore_wait(barrier, REG - 1)
+
+    def send_freq(step, carry):
+        peer = lax.rem(me + step, REG)
+        pltpu.make_async_remote_copy(
+            freq_in_ref, freq_ref.at[me], freq_send, freq_recv,
+            device_id=(peer,), device_id_type=MESH_ID,
+        ).start()
+        return carry
+
+    lax.fori_loop(1, REG, send_freq, 0)
+
+    counter = [0]
+    sends = []
+
+    def new_id():
+        counter[0] += 1
+        return counter[0] - 1
+
+    def device(axis, delta):
+        return me + (lax.rem(pos[axis] + delta, 4) - pos[axis]) * STRIDES[axis]
+
+    def view(where, parity, rows):
+        return nets_ref.at[where[0], where[1], where[2], parity, rows, :]
+
+    def start(src, dst, peer, number):
+        copy = pltpu.make_async_remote_copy(
+            src, dst, send_sem.at[number], recv_sem.at[number],
+            device_id=(peer,), device_id_type=MESH_ID,
+        )
+        copy.start()
+        sends.append(copy)
+
+    def arrive(dst, number):
+        pltpu.make_async_remote_copy(
+            dst, dst, send_sem.at[number], recv_sem.at[number],
+            device_id=(sibling,), device_id_type=MESH_ID,
+        ).wait_recv()
+
+    home = {0: pos[0], 1: pos[1], 2: pos[2]}
+    sibling_waits = []
+
+    def to_sibling(where, rows):
+        number = new_id()
+        start(view(where, core, rows), view(where, core, rows), sibling, number)
+        sibling_waits.append((view(where, 1 - core, rows), number))
+
+    whole = pl.ds(0, 4)
+
+    def make_stream(t):
+        a, b, c = ORDERS[t]
+        rows = pl.ds(96 * t, 96)
+        near = pl.ds(96 * t, 48)
+        far = pl.ds(96 * t + 48, 48)
+        base = dict(home)
+        left = {axis: lax.rem(pos[axis] + 3, 4) for axis in range(3)}
+        right = {axis: lax.rem(pos[axis] + 1, 4) for axis in range(3)}
+        opposite = {axis: lax.rem(pos[axis] + 2, 4) for axis in range(3)}
+
+        def spec(**kw):
+            out = dict(base)
+            for key, value in kw.items():
+                out[{"a": a, "b": b, "c": c}[key]] = value
+            return out
+
+        ids = {}
+
+        def send(name, axis, delta, where, part=rows, src=None):
+            number = new_id()
+            source = view(where, core, part) if src is None else src
+            start(source, view(where, core, part), device(axis, delta), number)
+            ids[name] = number
+
+        def wait(name, where, part=rows):
+            arrive(view(where, core, part), ids[name])
+
+        def stage0():
+            mine = payload_ref.at[rows, :]
+            send("A+", a, 1, spec(), src=mine)
+            send("A-", a, 3, spec(), src=mine)
+            send("B+o", b, 1, spec(), src=mine)
+            send("B-o", b, 3, spec(), src=mine)
+            send("C+o", c, 1, spec(), src=mine)
+            send("C-o", c, 3, spec(), src=mine)
+
+        def spread(where, tag):
+            send("B+" + tag, b, 1, where)
+            send("B-" + tag, b, 3, where)
+            send("C+" + tag, c, 1, where)
+            send("C-" + tag, c, 3, where)
+
+        def stage1():
+            low, high = spec(a=left[a]), spec(a=right[a])
+            wait("A+", low)
+            send("H+", a, 1, low, near)
+            spread(low, "l")
+            wait("A-", high)
+            send("H-", a, 3, high, far)
+            spread(high, "r")
+            to_sibling(low, rows)
+            to_sibling(high, rows)
+
+        def stage2():
+            across = spec(a=opposite[a])
+            wait("H+", across, near)
+            wait("H-", across, far)
+            spread(across, "d")
+            to_sibling(across, rows)
+
+        def line_arrivals(prefix, **kw):
+            wait(prefix + "o", spec(**kw))
+            wait(prefix + "l", spec(a=left[a], **kw))
+            wait(prefix + "r", spec(a=right[a], **kw))
+            wait(prefix + "d", spec(a=opposite[a], **kw))
+
+        def stage3():
+            line_arrivals("B+", b=left[b])
+            low = spec(a=whole, b=left[b])
+            send("BH+", b, 1, spec(a=pl.ds(0, 2), b=left[b]))
+            send("C+L", c, 1, low)
+            send("C-L", c, 3, low)
+            line_arrivals("B-", b=right[b])
+            high = spec(a=whole, b=right[b])
+            send("BH-", b, 3, spec(a=pl.ds(2, 2), b=right[b]))
+            send("C+R", c, 1, high)
+            send("C-R", c, 3, high)
+            to_sibling(low, rows)
+            to_sibling(high, rows)
+
+        def stage4():
+            wait("BH+", spec(a=pl.ds(0, 2), b=opposite[b]))
+            wait("BH-", spec(a=pl.ds(2, 2), b=opposite[b]))
+            across = spec(a=whole, b=opposite[b])
+            send("C+D", c, 1, across)
+            send("C-D", c, 3, across)
+            to_sibling(across, rows)
+
+        def stage5():
+            line_arrivals("C+", c=left[c])
+            send("CH+o", c, 1, spec(a=whole, c=left[c]))
+            line_arrivals("C-", c=right[c])
+            wait("C-R", spec(a=whole, b=right[b], c=right[c]))
+            send("CH-R", c, 3, spec(a=whole, b=right[b], c=right[c]))
+            wait("C+L", spec(a=whole, b=left[b], c=left[c]))
+            send("CH+L", c, 1, spec(a=whole, b=left[b], c=left[c]))
+            to_sibling(spec(a=whole, c=left[c]), rows)
+            to_sibling(spec(a=whole, c=right[c]), rows)
+            to_sibling(spec(a=whole, b=left[b], c=left[c]), rows)
+            to_sibling(spec(a=whole, b=right[b], c=right[c]), rows)
+
+        def stage6():
+            wait("C-D", spec(a=whole, b=opposite[b], c=right[c]))
+            send("CH-D", c, 3, spec(a=whole, b=opposite[b], c=right[c]))
+            wait("C+R", spec(a=whole, b=right[b], c=left[c]))
+            wait("C+D", spec(a=whole, b=opposite[b], c=left[c]))
+            wait("C-L", spec(a=whole, b=left[b], c=right[c]))
+            to_sibling(spec(a=whole, b=right[b], c=left[c]), rows)
+            to_sibling(spec(a=whole, b=opposite[b], c=left[c]), rows)
+            to_sibling(spec(a=whole, b=left[b], c=right[c]), rows)
+            to_sibling(spec(a=whole, b=opposite[b], c=right[c]), rows)
+
+        def stage7():
+            for name, line in (("CH+o", pos[b]), ("CH+L", left[b]), ("CH-R", right[b]), ("CH-D", opposite[b])):
+                where = spec(a=whole, b=line, c=opposite[c])
+                wait(name, where)
+                to_sibling(where, rows)
+
+        return (stage0, stage1, stage2, stage3, stage4, stage5, stage6, stage7)
+
+    streams = [make_stream(t) for t in range(3)]
+
+    def stage(number):
+        for stream in streams:
+            stream[number]()
+
+    stage(0)
+    own = new_id()
+    start(payload_ref, view(home, core, pl.ds(0, 288)), sibling, own)
+    sibling_waits.append((view(home, 1 - core, pl.ds(0, 288)), own))
+    keep = pltpu.make_async_copy(payload_ref, view(home, core, pl.ds(0, 288)), local_sem)
+    keep.start()
+
+    def features(first, count):
+        def body(step, carry):
+            turns = []
+            for j in range(GF):
+                b = step * GF + j
+                turns.append(features_of(freq_ref[table_ref[b]], coords_ref[pl.ds(b * 4, 4), :]))
+            for j in range(GF):
+                feature_ref[step * GF + j] = encode(turns[j])
+            return carry
+
+        lax.fori_loop(first, first + count, body, 0)
+        part = pl.ds(first * GF, count * GF)
+        copy = pltpu.make_async_copy(
+            feature_ref.at[part], feature_out_ref.at[part], feature_sem.at[first]
+        )
+        copy.start()
+        feature_copies.append(copy)
+
+    feature_copies = []
+    arrived = freq_ref.at[pl.ds(0, REG - 1)]
+    pltpu.make_async_copy(arrived, arrived, freq_recv).wait()
+    done = 0
+    for number in range(1, 8):
+        count = CHUNKS[number - 1]
+        if count:
+            features(done, count)
+        done += count
+        stage(number)
+    for ref, number in sibling_waits:
+        arrive(ref, number)
+    for copy in sends:
+        copy.wait_send()
+    pltpu.make_async_copy(arrived, arrived, freq_send).wait()
+    keep.wait()
+    for copy in feature_copies:
+        copy.wait()
 
 
 def tri(kind):
@@ -148,27 +393,61 @@
 
 
 def render_kernel(
-    table_ref, coords_ref, picks_ref, colour_grad_ref, feature_ref, hidden_w_ref, head_ref,
-    rendered_ref, grad_ref, hidden_ref, raw_ref,
+    table_ref, coords_ref, picks_ref, colour_grad_ref, feature_hbm_ref, nets_hbm_ref,
+    rendered_ref, grad_ref, hidden_ref, raw_ref, feature_ref, nets_ref, feature_sem, nets_sem,
 ):
     total = table_ref[383]
 
-    def forward(b, carry):
-        region = table_ref[b]
-        hid = jnp.maximum(dot(hidden_w_ref[region], feature_ref[b]), 0.0).astype(BF16)
-        hidden_ref[b] = hid
-        raw_ref[pl.ds(b * 8, 8), :] = dot(head_ref[region], hid)
+    def net_copy(part):
+        rows = pl.ds(part * 32, 32)
+        return pltpu.make_async_copy(nets_hbm_ref.at[rows], nets_ref.at[rows], nets_sem.at[part])
+
+    def feature_copy(step):
+        rows = pl.ds(step * GR, GR)
+        return pltpu.make_async_copy(feature_hbm_ref.at[rows], feature_ref.at[rows], feature_sem.at[step])
+
+    for part in range(4):
+        net_copy(part).start()
+        for step in range(NB // GR):
+            if step * 4 // (NB // GR) == part:
+                feature_copy(step).start()
+
+    groups = lax.div(total + (GR - 1), GR)
+
+    def forward(step, carry):
+        feature_copy(step).wait()
+        hids = []
+        for j in range(GR):
+            b = step * GR + j
+            hid = dot(nets_ref[table_ref[b], 0:HID, :], feature_ref[b])
+            hid = jnp.maximum(hid, 0.0).astype(BF16)
+            hidden_ref[b] = hid
+            hids.append(hid)
+        for j in range(GR):
+            b = step * GR + j
+            region = table_ref[b]
+            head = jnp.concatenate(
+                [nets_ref[region, HID:HID + 16, :], nets_ref[region, HID + 16:HID + 32, :]], axis=1
+            )
+            raw_ref[pl.ds(b * 8, 8), :] = dot(head, hids[j])[0:8]
         return carry
 
-    def blank(b, carry):
-        raw_ref[pl.ds(b * 8, 8), :] = jnp.zeros((8, LANES), F32)
+    def blank(step, carry):
+        feature_copy(step).wait()
+        for j in range(GR):
+            raw_ref[pl.ds((step * GR + j) * 8, 8), :] = jnp.zeros((8, LANES), F32)
         return carry
 
-    lax.fori_loop(0, total, forward, 0)
-    lax.fori_loop(total, NB, blank, 0)
+    first = 0
+    for part in range(4):
+        net_copy(part).wait()
+        last = groups if part == 3 else lax.div(table_ref[380 + part], GR)
+        lax.fori_loop(first, last, forward, 0)
+        first = last
+    lax.fori_loop(groups, NB // GR, blank, 0)
 
     raw = [raw_ref[pl.ds(o, NB, stride=8), :] for o in range(4)]
-    spacing = coords_ref[pl.ds(3, NB, stride=8), :]
+    spacing = coords_ref[pl.ds(3, NB, stride=4), :]
     soft = jnp.maximum(raw[0], 0.0) + jnp.log1p(jnp.exp(-jnp.abs(raw[0])))
     colour = [1.0 / (1.0 + jnp.exp(-raw[c])) for c in (1, 2, 3)]
     gate = 1.0 / (1.0 + jnp.exp(-raw[0]))
@@ -239,13 +518,17 @@
         raw_ref[pl.ds(o, NB, stride=8), :] = jnp.zeros((NB, LANES), F32)
     grad_ref[...] = jnp.zeros_like(grad_ref)
 
-    def backward(b, carry):
-        region = table_ref[b]
-        rg = raw_ref[pl.ds(b * 8, 8), :].astype(BF16)
-        grad_ref[region] += dot(rg, hidden_ref[b], ((1,), (1,)))
+    def backward(step, carry):
+        parts = []
+        for j in range(GR):
+            b = step * GR + j
+            rg = raw_ref[pl.ds(b * 8, 8), :].astype(BF16)
+            parts.append(dot(rg, hidden_ref[b], ((1,), (1,))))
+        for j in range(GR):
+            grad_ref[table_ref[step * GR + j]] += parts[j]
         return carry
 
-    lax.fori_loop(0, total, backward, 0)
+    lax.fori_loop(0, groups, backward, 0)
 
 
 def exact_dot_last(after):
@@ -264,7 +547,7 @@
         sort_kernel,
         out_shape=(
             jax.ShapeDtypeStruct((4, NB, SEG), BF16),
-            jax.ShapeDtypeStruct((NB * 8, LANES), F32),
+            jax.ShapeDtypeStruct((NB * 4, LANES), F32),
             jax.ShapeDtypeStruct((1, 384), jnp.int32),
         ),
         in_specs=[VM, VM, VM],
@@ -273,49 +556,60 @@
     )(crossed_row, sample_points, sample_spacing)
 
 
-def make_features(table, coords, freq_all):
+def gather_nets(table, coords, freq4, hidden, head32):
     return pl.pallas_call(
-        feature_kernel,
-        out_shape=jax.ShapeDtypeStruct((NB, LANES, LANES), BF16),
-        in_specs=[SM, VM, VM],
-        out_specs=VM,
-        compiler_params=params(40),
-    )(table, coords, freq_all)
-
-
-def render_all(table, coords, picks, colour_grad, feature, hidden_all, head_all):
+        gather_kernel,
+        out_shape=(
+            jax.ShapeDtypeStruct((4, 4, 4, 2, HID + 32, LANES), BF16),
+            jax.ShapeDtypeStruct((NB, LANES, LANES), BF16),
+        ),
+        in_specs=[SM, VM, VM, VM, VM],
+        out_specs=(ANY, ANY),
+        scratch_shapes=[
+            pltpu.VMEM((HID + 32, LANES), BF16),
+            pltpu.VMEM((REG, 4, LANES), F32),
+            pltpu.VMEM((NB, LANES, LANES), BF16),
+            pltpu.SemaphoreType.DMA((COPIES,)),
+            pltpu.SemaphoreType.DMA((COPIES,)),
+            pltpu.SemaphoreType.DMA,
+            pltpu.SemaphoreType.DMA,
+            pltpu.SemaphoreType.DMA,
+            pltpu.SemaphoreType.DMA((NB // GF,)),
+        ],
+        compiler_params=params(40, collective_id=0, has_side_effects=True),
+    )(table, coords, freq4, hidden, head32)
+
+
+def render_all(table, coords, picks, colour_grad, feature, nets):
     return pl.pallas_call(
         render_kernel,
         out_shape=(
             jax.ShapeDtypeStruct((3, RAYS), F32),
             jax.ShapeDtypeStruct((REG, 8, HID), F32),
         ),
-        in_specs=[SM, VM, VM, VM, VM, VM, VM],
+        in_specs=[SM, VM, VM, VM, ANY, ANY],
         out_specs=(VM, VM),
         scratch_shapes=[
             pltpu.VMEM((NB, HID, LANES), BF16),
             pltpu.VMEM((NB * 8, LANES), F32),
+            pltpu.VMEM((NB, LANES, LANES), BF16),
+            pltpu.VMEM((REG, HID + 32, LANES), BF16),
+            pltpu.SemaphoreType.DMA((NB // GR,)),
+            pltpu.SemaphoreType.DMA((4,)),
         ],
         compiler_params=params(60),
-    )(table, coords, picks, colour_grad, feature, hidden_all, head_all)
-
-
-def local_part(sample_points, sample_spacing, crossed, colour_grad, freq_all, hidden_all, head_all):
+    )(table, coords, picks, colour_grad, feature, nets)
+
+
+def on_device(sample_points, sample_spacing, crossed, colour_grad, freq, w_hidden, w_head):
+    freq4 = jnp.pad(freq[0].astype(F32), ((0, 1), (0, LANES - FREQ)))
+    halves = w_head[0].reshape(4, 2, LANES).transpose(1, 0, 2)
+    head32 = jnp.pad(halves, ((0, 0), (0, 12), (0, 0))).reshape(32, LANES)
     picks, coords, table = sort_segments(sample_points, sample_spacing, crossed)
     table = table.reshape(384)
-    feature = make_features(table, coords, freq_all)
-    return render_all(table, coords, picks, colour_grad, feature, hidden_all, head_all)
-
-
-def on_device(sample_points, sample_spacing, crossed, colour_grad, freq, w_hidden, w_head):
-    freq8 = jnp.pad(freq[0].astype(F32), ((0, 5), (0, LANES - FREQ)))
-    head8 = jnp.pad(w_head[0], ((0, 4), (0, 0)))
-    freq_all = lax.all_gather(freq8, "region")
-    hidden_all = lax.all_gather(w_hidden[0].T, "region")
-    head_all = lax.all_gather(head8, "region")
-    rendered, grad = local_part(
-        sample_points, sample_spacing, crossed, colour_grad, freq_all, hidden_all, head_all
-    )
+    nets, feature = gather_nets(table, coords, freq4, w_hidden[0], head32)
+    nets = nets.reshape(REG, HID + 32, LANES)
+    rendered, grad = render_all(table, coords, picks, colour_grad, feature, nets)
     parts = lax.all_to_all(grad[:, :4], "region", split_axis=0, concat_axis=0, tiled=True)
     return rendered, jnp.sum(parts, axis=0, keepdims=True)
 

time: 328 us -> 117 us (0.36)
  Pallas kernels: 192 us -> 82 us
  blocking collectives: 95.9 us -> 21.4 us
  between operations: 14.1 us -> 0.69 us
  local copies, waits for them, and re-layouts: 22.8 us -> 10.9 us
    pallas_call x1, Pallas kernels: 146 us -> 30.1 us  [render_all(): pl.pallas_call(render_kernel, out_shape=(jax.ShapeDtypeStruct((3, RAYS),...]
    all_gather x2 -> x0, blocking collectives: 76.2 us -> none  [the longest x1 39.9 us: on_device(): freq_all = lax.all_gather(freq8, 'region')]
    all_gather x1 -> x0, local copies, waits for them, and re-layouts: 11.9 us -> none  [on_device(): hidden_all = lax.all_gather(w_hidden[0].T, 'region')]
    pallas_call x1, Pallas kernels: 43.1 us -> 49 us  [gather_nets(): pl.pallas_call(gather_kernel, out_shape=(jax.ShapeDtypeStruct((4, 4, 4, 2...]
    unnamed x12 -> x14, local copies, waits for them, and re-layouts: 8.87 us -> 8.89 us
  transfers between devices with their start and end apart: 1 -> 0, of which waited for: 0 -> 0; matrix products, arithmetic and copies ran while one was open for 1% -> 0% of each run, Pallas kernels for 14% -> 0%
where the time goes in v2:
time: 117 us; the launch traced here: 116 us
  Pallas kernels  82 us (70%)
  blocking collectives  21.4 us (18%)
  local copies, waits for them, and re-layouts  10.9 us (9%)
  other arithmetic  1.44 us (1%)
    pallas_call x1, Pallas kernels, gather_nets(): pl.pallas_call(gather_kernel, out_shape=(jax.ShapeDtypeStruct((4, 4, 4, 2...  49 us
    pallas_call x1, Pallas kernels, render_all(): pl.pallas_call(render_kernel, out_shape=(jax.ShapeDtypeStruct((3, RAYS),...  30.1 us
    all_to_all x1, blocking collectives, on_device(): lax.all_to_all(grad[:, :4], 'region', split_axis=0, concat_axis=0, tiled=...  21.4 us
    unnamed x14, local copies, waits for them, and re-layouts  8.89 us
    pallas_call x1, Pallas kernels, sort_segments(): pl.pallas_call(sort_kernel, out_shape=(jax.ShapeDtypeStruct((4, NB, SEG),...  2.9 us

profile of v2, /device:TPU:1, one launch (start us, length us, event | category | flops | bytes accessed | tf_op | source)
XLA Modules:
  0.0 116.4 jit_solution(12883014943496526942)
XLA Ops:
  0.6 0.7 pad_convert_fusion.freq_in_ref
  1.3 0.7 copy.11
  2.0 1.3 %copy.9.points_ref = f32[256,3,128]{2,1,0:T(4,128)S(1)} copy(f32[256,3,128]{2,0,1:T(8,128)} %param.7) | data formatting | bytes 786432 | tf_op args[0]
  3.3 0.7 pad.12
  4.0 0.0 copy-start.3
  4.0 0.9 copy-done.3
  4.9 2.9 %shard_map.86 = (bf16[4,352,1024]{2,1,0:T(8,128)(2,1)S(1)}, f32[1408,128]{1,0:T(8,128)S(1)}, s32[1,384]{1,0:T(1,128)S(1)}) custom-call(s32[1,1024]{1,0:T(1,128)S(1)} %bitcast.15, f32[256,3,128]{2,1,0:T(4,128)S(1)} %copy.9.points_ref, f32[256,128]{1,0:T(8,128)S(1)} %copy-done.3), custom_call_target="tpu_custom_call" | custom-call | tf_op jit(solution)/shard_map/pallas_call | solution.py:546
  7.8 0.0 copy-start.2
  7.8 1.6 %copy-done.2 = bf16[4,352,1024]{2,1,0:T(8,128)(2,1)} copy-done((bf16[4,352,1024]{2,1,0:T(8,128)(2,1)}, bf16[4,352,1024]{2,1,0:T(8,128)(2,1)S(1)}, u32[]{:S(2)}) %copy-start.2) | copy-done | bytes 2883608
  9.4 0.0 copy-start.1
  9.4 0.0 copy-start.5
  9.4 0.0 copy-start.4
  9.4 0.9 copy-done.4
  10.3 49.0 %shard_map.87 = (bf16[4,4,4,2,288,128]{5,4,3,2,1,0:T(8,128)(2,1)S(1)}, bf16[352,128,128]{2,1,0:T(8,128)(2,1)}) custom-call(s32[384]{0:T(512)S(1)} %reduce.table_ref, f32[1408,128]{1,0:T(8,128)S(1)} %get-tuple-element.10.coords_ref, f32[4,128]{1,0:T(4,128)S(1)} %pad_convert_fusion.freq_in_ref, bf16[128,256]{1,0:T(8,128)(2,1)S(1)} %bitcast.13, ...), custom_call_target="tpu_custom_call" | custom-call | tf_op jit(solution)/shard_map/pallas_call | solution.py:560
  59.4 0.0 copy-start
  59.4 3.5 %copy-done = bf16[4,4,4,2,288,128]{5,4,3,2,1,0:T(8,128)(2,1)} copy-done((bf16[4,4,4,2,288,128]{5,4,3,2,1,0:T(8,128)(2,1)}, bf16[4,4,4,2,288,128]{5,4,3,2,1,0:T(8,128)(2,1)S(1)}, u32[]{:S(2)}) %copy-start) | copy-done | bytes 9437208
  62.9 0.0 copy-done.1
  62.9 0.0 copy-done.5
  62.9 30.1 %shard_map.88 = (f32[3,256]{1,0:T(4,128)}, f32[128,8,256]{2,1,0:T(8,128)}) custom-call(s32[384]{0:T(512)} %copy-done.5, f32[1408,128]{1,0:T(8,128)} %copy-done.1, bf16[4,352,1024]{2,1,0:T(8,128)(2,1)} %copy-done.2, f32[3,256]{1,0:T(4,128)} %colour_grad_ref.1, bf16[352,128,128]{2,1,0:T(8,128)(2,1)} %get-tuple-element.12.feature_hbm_ref, ...), custom_call_target="tpu_custom_call" | custom-call | tf_op jit(solution)/shard_map/pallas_call | solution.py:584
  93.0 1.3 %slice.3 = f32[128,4,256]{2,1,0:T(4,128)S(1)} slice(f32[128,8,256]{2,1,0:T(8,128)} %get-tuple-element.15), slice={[0:128], [0:4], [0:256]} | slice | bytes 1048576 | tf_op jit(solution)/shard_map/slice | solution.py:613
  94.3 21.4 %all_to_all.5 = f32[128,4,256]{2,1,0:T(4,128)S(1)} all-to-all(f32[128,4,256]{2,1,0:T(4,128)S(1)} %slice.3), channel_id=1, replica_groups=mesh['region'=128] {'region'}, dimensions={0} | all-to-all | bytes 1048576 | tf_op jit(solution)/shard_map/all_to_all | solution.py:613
  115.7 0.7 reduce_sum.9
  (1 shorter events, 0.0 us)
Async XLA Ops:
  4.0 0.9 copy-start.3
  7.8 1.6 %copy-start.2 = (bf16[4,352,1024]{2,1,0:T(8,128)(2,1)}, bf16[4,352,1024]{2,1,0:T(8,128)(2,1)S(1)}, u32[]{:S(2)}) copy-start(bf16[4,352,1024]{2,1,0:T(8,128)(2,1)S(1)} %get-tuple-element.11.picks_ref) | copy-start | bytes 8650756
  9.4 53.5 %copy-start.1 = (f32[1408,128]{1,0:T(8,128)}, f32[1408,128]{1,0:T(8,128)S(1)}, u32[]{:S(2)}) copy-start(f32[1408,128]{1,0:T(8,128)S(1)} %get-tuple-element.10.coords_ref) | copy-start | bytes 2162692
  9.4 53.5 %copy-start.5 = (s32[384]{0:T(512)}, s32[384]{0:T(512)S(1)}, u32[]{:S(2)}) copy-start(s32[384]{0:T(512)S(1)} %reduce.table_ref) | copy-start | bytes 4612
  9.4 0.9 copy-start.4
  59.4 3.5 %copy-start = (bf16[4,4,4,2,288,128]{5,4,3,2,1,0:T(8,128)(2,1)}, bf16[4,4,4,2,288,128]{5,4,3,2,1,0:T(8,128)(2,1)S(1)}, u32[]{:S(2)}) copy-start(bf16[4,4,4,2,288,128]{5,4,3,2,1,0:T(8,128)(2,1)S(1)} %get-tuple-element.13) | copy-start | bytes 28311556

commit v3 on v2

--- a/solution.py
+++ b/solution.py
@@ -19,15 +19,17 @@
 LANES = 128
 COPIES = 152
 GF = 32
-CHUNKS = (1, 1, 2, 2, 2, 2, 1)
+CHUNKS = (4, 3, 2, 1, 1)
 GR = 16
 
 F32 = jnp.float32
 BF16 = jnp.bfloat16
+FREQ_TYPE = BF16
 
 SIN_C = (4.44288292, -7.3082457, 3.60635441, -0.84611289, 0.10982699)
 COS_C = (1.4142135, -6.97885099, 5.73946117, -1.88356298, 0.31069819)
 
+HBM = pl.BlockSpec(memory_space=pltpu.HBM)
 VM = pl.BlockSpec(memory_space=pltpu.VMEM)
 SM = pl.BlockSpec(memory_space=pltpu.SMEM)
 ANY = pl.BlockSpec(memory_space=pl.ANY)
@@ -61,8 +63,8 @@
     return out
 
 
-def sort_kernel(crossed_ref, points_ref, spacing_ref, picks_ref, coords_ref, table_ref):
-    owner = crossed_ref[...]
+def sort_places(crossed):
+    owner = jnp.concatenate([crossed[k:k + 1] for k in range(K)], axis=1)
     onehot = (iota((REG, SEG), 0) == owner).astype(F32)
     onehot16 = onehot.astype(BF16)
     earlier = (iota((SEG, SEG), 0) < iota((SEG, SEG), 1)).astype(F32).astype(BF16)
@@ -76,7 +78,6 @@
     start_row = jnp.sum(onehot * starts, axis=0, keepdims=True)
     step = jnp.floor(rank_row * 0.25)
     place = (rank_row - 4.0 * step) * NB + start_row + step
-    place = place.astype(jnp.int32)
     block_at = iota((REG, 384), 1).astype(F32)
     owner_of = jnp.sum((block_at >= ends).astype(F32), axis=0, keepdims=True)
     owner_of = jnp.minimum(owner_of, REG - 1.0)
@@ -85,10 +86,11 @@
     for part in range(3):
         bound = ends[(part + 1) * 32 - 1:(part + 1) * 32]
         table = jnp.where(iota((1, 384), 1) == 380 + part, bound, table)
-    table_ref[...] = table.astype(jnp.int32)
-
+    return place.astype(jnp.int32), table.astype(jnp.int32)
+
+
+def sort_sources(sources):
     lane_group = iota((RAYS, LANES), 1) // S
-    sources = [points_ref[:, 0, :], points_ref[:, 1, :], points_ref[:, 2, :], spacing_ref[...]]
     rows = []
     for k in range(K):
         row = jnp.zeros((RAYS, LANES), F32)
@@ -99,14 +101,14 @@
             row = jnp.where(lane_group == c, moved, row)
         rows.append(row)
     packed = jnp.concatenate(rows, axis=0)
-    hi, mid, low = pieces(packed)
-    source = jnp.concatenate([hi, mid, low], axis=1)
+    return jnp.concatenate(pieces(packed), axis=1)
+
+
+def sort_coords(picks_ref, source, coords_ref):
     block_group = iota((NB, LANES), 1) // S
     coords = [jnp.zeros((NB, LANES), F32) for _ in range(4)]
     for q in range(4):
-        picks = (iota((NB, SEG), 0) + q * NB == place).astype(F32).astype(BF16)
-        picks_ref[q] = picks
-        three = dot(picks, source)
+        three = dot(picks_ref[q], source)
         got = three[:, :128] + three[:, 128:256] + three[:, 256:]
         for c in range(4):
             moved = got
@@ -116,9 +118,15 @@
     for c in range(4):
         value = coords[c] * np.float32(0.5 / np.pi) if c < 3 else coords[c]
         coords_ref[pl.ds(c, NB, stride=4), :] = value
+    return coords[3]
+
+
+def bounded(region):
+    return jnp.maximum(jnp.minimum(region, REG - 1), 0)
 
 
 def features_of(freq, coords):
+    freq = freq.astype(F32)
     f12 = jnp.concatenate([freq, freq, freq], axis=0).astype(BF16)
     hi = coords.astype(BF16).astype(F32)
     mid = (coords - hi).astype(BF16).astype(F32)
@@ -140,37 +148,76 @@
 MESH_ID = pl.DeviceIdType.MESH
 
 
+def greet(barrier, me):
+    base, inner, outer = me - lax.rem(me, 8), lax.rem(me, 8), lax.div(me, 8)
+
+    def within(step, carry):
+        peer = base + lax.rem(inner + step, 8)
+        pl.semaphore_signal(barrier, inc=1, device_id=(peer,), device_id_type=MESH_ID)
+        return carry
+
+    def across(step, carry):
+        peer = lax.rem(outer + step, 16) * 8 + inner
+        pl.semaphore_signal(barrier, inc=1, device_id=(peer,), device_id_type=MESH_ID)
+        return carry
+
+    lax.fori_loop(1, 8, within, 0)
+    lax.fori_loop(1, 16, across, 0)
+
+
 def gather_kernel(
-    table_ref, coords_ref, freq_in_ref, hidden_in_ref, head_in_ref, nets_ref, feature_out_ref,
-    payload_ref, freq_ref, feature_ref,
-    send_sem, recv_sem, freq_send, freq_recv, local_sem, feature_sem,
+    crossed_hbm, points_hbm, spacing_hbm, freq_hbm, hidden_hbm, head_hbm,
+    nets_ref, feature_out_ref, picks_out_ref, spacing_out_ref, table_out_ref,
+    payload_ref, freq_ref, feature_ref, picks_ref, coords_ref, table_ref,
+    crossed_ref, points_ref, spacing_ref, freq_in_ref, hidden_in_ref, head_in_ref,
+    send_sem, recv_sem, freq_send, freq_recv, local_sem, feature_sem, input_sem,
 ):
     me = lax.axis_index("region")
     core = lax.rem(me, 2)
     sibling = me + 1 - 2 * core
     pos = [lax.rem(lax.div(me, stride), 4) for stride in STRIDES]
+    base, inner, outer = me - lax.rem(me, 8), lax.rem(me, 8), lax.div(me, 8)
     barrier = pltpu.get_barrier_semaphore()
-
-    def greet(step, carry):
-        peer = lax.rem(me + step, REG)
-        pl.semaphore_signal(barrier, inc=1, device_id=(peer,), device_id_type=MESH_ID)
-        return carry
-
-    lax.fori_loop(1, REG, greet, 0)
+    inputs = [
+        pltpu.make_async_copy(src, dst, input_sem.at[number])
+        for number, (src, dst) in enumerate((
+            (hidden_hbm, hidden_in_ref), (freq_hbm, freq_in_ref), (head_hbm, head_in_ref),
+            (crossed_hbm, crossed_ref), (points_hbm, points_ref), (spacing_hbm, spacing_ref),
+        ))
+    ]
+    for copy in inputs:
+        copy.start()
+    greet(barrier, me)
+    for copy in inputs[:3]:
+        copy.wait()
     payload_ref[0:HID, :] = hidden_in_ref[...].astype(F32).T.astype(BF16)
-    payload_ref[HID:HID + 32, :] = head_in_ref[...]
-    freq_ref[me] = freq_in_ref[...]
-    pl.semaphore_wait(barrier, REG - 1)
-
-    def send_freq(step, carry):
-        peer = lax.rem(me + step, REG)
+    head = head_in_ref[...].astype(F32)
+    blank = jnp.zeros((12, LANES), F32)
+    head = jnp.concatenate([head[:, :LANES], blank, head[:, LANES:], blank], axis=0)
+    payload_ref[HID:HID + 32, :] = head.astype(BF16)
+    freq_in = jnp.concatenate([freq_in_ref[...].astype(F32), jnp.zeros((3, FREQ), F32)], axis=1)
+    freq_in = jnp.concatenate([freq_in, jnp.zeros((1, LANES), F32)], axis=0)
+    freq_ref[me] = freq_in.astype(FREQ_TYPE)
+    pl.semaphore_wait(barrier, 22)
+
+    def freq_within(step, carry):
+        peer = base + lax.rem(inner + step, 8)
         pltpu.make_async_remote_copy(
-            freq_in_ref, freq_ref.at[me], freq_send, freq_recv,
+            freq_ref.at[me], freq_ref.at[me], freq_send.at[0], freq_recv.at[0],
             device_id=(peer,), device_id_type=MESH_ID,
         ).start()
         return carry
 
-    lax.fori_loop(1, REG, send_freq, 0)
+    def freq_across(step, carry):
+        peer = lax.rem(outer + step, 16) * 8 + inner
+        rows = pl.ds(base, 8)
+        pltpu.make_async_remote_copy(
+            freq_ref.at[rows], freq_ref.at[rows], freq_send.at[1], freq_recv.at[1],
+            device_id=(peer,), device_id_type=MESH_ID,
+        ).start()
+        return carry
+
+    lax.fori_loop(1, 8, freq_within, 0)
 
     counter = [0]
     sends = []
@@ -347,7 +394,7 @@
             turns = []
             for j in range(GF):
                 b = step * GF + j
-                turns.append(features_of(freq_ref[table_ref[b]], coords_ref[pl.ds(b * 4, 4), :]))
+                turns.append(features_of(freq_ref[bounded(table_ref[0, b])], coords_ref[pl.ds(b * 4, 4), :]))
             for j in range(GF):
                 feature_ref[step * GF + j] = encode(turns[j])
             return carry
@@ -361,21 +408,40 @@
         feature_copies.append(copy)
 
     feature_copies = []
-    arrived = freq_ref.at[pl.ds(0, REG - 1)]
-    pltpu.make_async_copy(arrived, arrived, freq_recv).wait()
+    inputs[3].wait()
+    place, table = sort_places(crossed_ref[...])
+    table_out_ref[...] = table
+    table_copy = pltpu.make_async_copy(table_out_ref, table_ref, input_sem.at[6])
+    table_copy.start()
+    seven, many = freq_ref.at[pl.ds(0, 7)], freq_ref.at[pl.ds(0, 120)]
+    pltpu.make_async_copy(seven, seven, freq_recv.at[0]).wait()
+    lax.fori_loop(1, 16, freq_across, 0)
+    stage(1)
+    for q in range(4):
+        picks_ref[q] = (iota((NB, SEG), 0) + q * NB == place).astype(F32).astype(BF16)
+    picks_copy = pltpu.make_async_copy(picks_ref, picks_out_ref, input_sem.at[7])
+    picks_copy.start()
+    inputs[4].wait()
+    inputs[5].wait()
+    source = sort_sources([points_ref[0], points_ref[1], points_ref[2], spacing_ref[...]])
+    stage(2)
+    spacing_out_ref[...] = sort_coords(picks_ref, source, coords_ref)
+    table_copy.wait()
+    pltpu.make_async_copy(many, many, freq_recv.at[1]).wait()
     done = 0
-    for number in range(1, 8):
-        count = CHUNKS[number - 1]
-        if count:
-            features(done, count)
+    for number in range(3, 8):
+        count = CHUNKS[number - 3]
+        features(done, count)
         done += count
         stage(number)
     for ref, number in sibling_waits:
         arrive(ref, number)
     for copy in sends:
         copy.wait_send()
-    pltpu.make_async_copy(arrived, arrived, freq_send).wait()
+    pltpu.make_async_copy(seven, seven, freq_send.at[0]).wait()
+    pltpu.make_async_copy(many, many, freq_send.at[1]).wait()
     keep.wait()
+    picks_copy.wait()
     for copy in feature_copies:
         copy.wait()
 
@@ -393,10 +459,11 @@
 
 
 def render_kernel(
-    table_ref, coords_ref, picks_ref, colour_grad_ref, feature_hbm_ref, nets_hbm_ref,
-    rendered_ref, grad_ref, hidden_ref, raw_ref, feature_ref, nets_ref, feature_sem, nets_sem,
+    table_ref, spacing_ref, colour_grad_ref, picks_hbm_ref, feature_hbm_ref, nets_hbm_ref,
+    rendered_ref, grad_ref, hidden_ref, raw_ref, feature_ref, nets_ref, picks_ref,
+    feature_sem, nets_sem, picks_sem,
 ):
-    total = table_ref[383]
+    total = table_ref[0, 383]
 
     def net_copy(part):
         rows = pl.ds(part * 32, 32)
@@ -412,6 +479,8 @@
             if step * 4 // (NB // GR) == part:
                 feature_copy(step).start()
 
+    picks_copy = pltpu.make_async_copy(picks_hbm_ref, picks_ref, picks_sem)
+    picks_copy.start()
     groups = lax.div(total + (GR - 1), GR)
 
     def forward(step, carry):
@@ -419,13 +488,13 @@
         hids = []
         for j in range(GR):
             b = step * GR + j
-            hid = dot(nets_ref[table_ref[b], 0:HID, :], feature_ref[b])
+            hid = dot(nets_ref[table_ref[0, b], 0:HID, :], feature_ref[b])
             hid = jnp.maximum(hid, 0.0).astype(BF16)
             hidden_ref[b] = hid
             hids.append(hid)
         for j in range(GR):
             b = step * GR + j
-            region = table_ref[b]
+            region = table_ref[0, b]
             head = jnp.concatenate(
                 [nets_ref[region, HID:HID + 16, :], nets_ref[region, HID + 16:HID + 32, :]], axis=1
             )
@@ -441,13 +510,14 @@
     first = 0
     for part in range(4):
         net_copy(part).wait()
-        last = groups if part == 3 else lax.div(table_ref[380 + part], GR)
+        last = groups if part == 3 else lax.div(table_ref[0, 380 + part], GR)
         lax.fori_loop(first, last, forward, 0)
         first = last
     lax.fori_loop(groups, NB // GR, blank, 0)
 
     raw = [raw_ref[pl.ds(o, NB, stride=8), :] for o in range(4)]
-    spacing = coords_ref[pl.ds(3, NB, stride=4), :]
+    spacing = spacing_ref[...]
+    picks_copy.wait()
     soft = jnp.maximum(raw[0], 0.0) + jnp.log1p(jnp.exp(-jnp.abs(raw[0])))
     colour = [1.0 / (1.0 + jnp.exp(-raw[c])) for c in (1, 2, 3)]
     gate = 1.0 / (1.0 + jnp.exp(-raw[0]))
@@ -525,7 +595,9 @@
             rg = raw_ref[pl.ds(b * 8, 8), :].astype(BF16)
             parts.append(dot(rg, hidden_ref[b], ((1,), (1,))))
         for j in range(GR):
-            grad_ref[table_ref[step * GR + j]] += parts[j]
+            region = table_ref[0, step * GR + j]
+            grad_ref[0, region] += parts[j][0:4, :LANES]
+            grad_ref[1, region] += parts[j][0:4, LANES:]
         return carry
 
     lax.fori_loop(0, groups, backward, 0)
@@ -541,77 +613,154 @@
     return pltpu.CompilerParams(vmem_limit_bytes=mib * 1024 * 1024, **kw)
 
 
-def sort_segments(sample_points, sample_spacing, crossed):
-    crossed_row = crossed.T.reshape(1, SEG)
-    return pl.pallas_call(
-        sort_kernel,
-        out_shape=(
-            jax.ShapeDtypeStruct((4, NB, SEG), BF16),
-            jax.ShapeDtypeStruct((NB * 4, LANES), F32),
-            jax.ShapeDtypeStruct((1, 384), jnp.int32),
-        ),
-        in_specs=[VM, VM, VM],
-        out_specs=(VM, VM, VM),
-        compiler_params=params(32),
-    )(crossed_row, sample_points, sample_spacing)
-
-
-def gather_nets(table, coords, freq4, hidden, head32):
+def gather_nets(crossed, points, spacing, freq, hidden, head):
     return pl.pallas_call(
         gather_kernel,
         out_shape=(
             jax.ShapeDtypeStruct((4, 4, 4, 2, HID + 32, LANES), BF16),
             jax.ShapeDtypeStruct((NB, LANES, LANES), BF16),
+            jax.ShapeDtypeStruct((4, NB, SEG), BF16),
+            jax.ShapeDtypeStruct((NB, LANES), F32),
+            jax.ShapeDtypeStruct((1, 384), jnp.int32),
         ),
-        in_specs=[SM, VM, VM, VM, VM],
-        out_specs=(ANY, ANY),
+        in_specs=[ANY] * 6,
+        out_specs=(HBM, HBM, HBM, VM, VM),
         scratch_shapes=[
             pltpu.VMEM((HID + 32, LANES), BF16),
-            pltpu.VMEM((REG, 4, LANES), F32),
+            pltpu.VMEM((REG, 4, LANES), FREQ_TYPE),
             pltpu.VMEM((NB, LANES, LANES), BF16),
+            pltpu.VMEM((4, NB, SEG), BF16),
+            pltpu.VMEM((NB * 4, LANES), F32),
+            pltpu.SMEM((1, 384), jnp.int32),
+            pltpu.VMEM((K, RAYS), jnp.int32),
+            pltpu.VMEM((3, RAYS, LANES), F32),
+            pltpu.VMEM((RAYS, LANES), F32),
+            pltpu.VMEM((3, FREQ), BF16),
+            pltpu.VMEM((LANES, HID), BF16),
+            pltpu.VMEM((4, HID), BF16),
             pltpu.SemaphoreType.DMA((COPIES,)),
             pltpu.SemaphoreType.DMA((COPIES,)),
-            pltpu.SemaphoreType.DMA,
-            pltpu.SemaphoreType.DMA,
+            pltpu.SemaphoreType.DMA((2,)),
+            pltpu.SemaphoreType.DMA((2,)),
             pltpu.SemaphoreType.DMA,
             pltpu.SemaphoreType.DMA((NB // GF,)),
+            pltpu.SemaphoreType.DMA((8,)),
         ],
-        compiler_params=params(40, collective_id=0, has_side_effects=True),
-    )(table, coords, freq4, hidden, head32)
-
-
-def render_all(table, coords, picks, colour_grad, feature, nets):
+        compiler_params=params(50, collective_id=0, has_side_effects=True),
+    )(crossed, points, spacing, freq, hidden, head)
+
+
+def render_all(table, spacing, colour_grad, picks, feature, nets):
     return pl.pallas_call(
         render_kernel,
         out_shape=(
             jax.ShapeDtypeStruct((3, RAYS), F32),
-            jax.ShapeDtypeStruct((REG, 8, HID), F32),
+            jax.ShapeDtypeStruct((2, REG, 4, LANES), F32),
         ),
-        in_specs=[SM, VM, VM, VM, ANY, ANY],
+        in_specs=[SM, VM, VM, HBM, HBM, HBM],
         out_specs=(VM, VM),
         scratch_shapes=[
             pltpu.VMEM((NB, HID, LANES), BF16),
             pltpu.VMEM((NB * 8, LANES), F32),
             pltpu.VMEM((NB, LANES, LANES), BF16),
             pltpu.VMEM((REG, HID + 32, LANES), BF16),
+            pltpu.VMEM((4, NB, SEG), BF16),
             pltpu.SemaphoreType.DMA((NB // GR,)),
             pltpu.SemaphoreType.DMA((4,)),
+            pltpu.SemaphoreType.DMA,
         ],
         compiler_params=params(60),
-    )(table, coords, picks, colour_grad, feature, nets)
+    )(table, spacing, colour_grad, picks, feature, nets)
+
+
+def reduce_kernel(
+    grad_ref, out_ref, got_a, sum_a, last_a, got_b, sum_b, last_b, send_sem, recv_sem
+):
+    me = lax.axis_index("region")
+    base, inner, outer = me - lax.rem(me, 8), lax.rem(me, 8), lax.div(me, 8)
+    barrier = pltpu.get_barrier_semaphore()
+    greet(barrier, me)
+    pl.semaphore_wait(barrier, 22)
+    within = lambda step: base + lax.rem(inner + step, 8)
+    across = lambda step: lax.rem(outer + step, 16) * 8 + inner
+
+    def copy(src, dst, number, peer):
+        return pltpu.make_async_remote_copy(
+            src, dst, send_sem.at[number], recv_sem.at[number],
+            device_id=(peer,), device_id_type=MESH_ID,
+        )
+
+    def each(count, first, make):
+        def body(step, carry):
+            make(step, first + step)
+            return carry
+
+        lax.fori_loop(1, count, body, 0)
+
+    sent_a = lambda step: grad_ref.at[0, :, lax.rem(inner + step, 8)]
+    sent_b = lambda step: grad_ref.at[1, lax.rem(outer + step, 16)]
+    each(8, 0, lambda step, n: copy(sent_a(step), got_a.at[step], n, within(step)).start())
+    each(16, 8, lambda step, n: copy(sent_b(step), got_b.at[step], n, across(step)).start())
+
+    def add_a(step, total):
+        copy(sent_a(step), got_a.at[step], step, within(step)).wait_recv()
+        return total + got_a[step]
+
+    sum_a[...] = lax.fori_loop(1, 8, add_a, grad_ref[0, :, inner])
+    part_a = lambda step: sum_a.at[lax.rem(outer + step, 16)]
+    each(16, 24, lambda step, n: copy(part_a(step), last_a.at[step], n, across(step)).start())
+
+    def add_b(step, total):
+        copy(sent_b(step), got_b.at[step], 8 + step, across(step)).wait_recv()
+        return total + got_b[step]
+
+    sum_b[...] = lax.fori_loop(1, 16, add_b, grad_ref[1, outer])
+    part_b = lambda step: sum_b.at[lax.rem(inner + step, 8)]
+    each(8, 40, lambda step, n: copy(part_b(step), last_b.at[step], n, within(step)).start())
+
+    def end_a(step, total):
+        copy(part_a(step), last_a.at[step], 24 + step, across(step)).wait_recv()
+        return total + last_a[step]
+
+    def end_b(step, total):
+        copy(part_b(step), last_b.at[step], 40 + step, within(step)).wait_recv()
+        return total + last_b[step]
+
+    out_ref[:, :LANES] = lax.fori_loop(1, 16, end_a, sum_a[outer])
+    out_ref[:, LANES:] = lax.fori_loop(1, 8, end_b, sum_b[inner])
+    each(8, 0, lambda step, n: copy(sent_a(step), got_a.at[step], n, within(step)).wait_send())
+    each(16, 8, lambda step, n: copy(sent_b(step), got_b.at[step], n, across(step)).wait_send())
+    each(16, 24, lambda step, n: copy(part_a(step), last_a.at[step], n, across(step)).wait_send())
+    each(8, 40, lambda step, n: copy(part_b(step), last_b.at[step], n, within(step)).wait_send())
+
+
+def reduce_heads(grad):
+    return pl.pallas_call(
+        reduce_kernel,
+        out_shape=jax.ShapeDtypeStruct((4, HID), F32),
+        in_specs=[VM],
+        out_specs=VM,
+        scratch_shapes=[
+            pltpu.VMEM((8, 16, 4, LANES), F32),
+            pltpu.VMEM((16, 4, LANES), F32),
+            pltpu.VMEM((16, 4, LANES), F32),
+            pltpu.VMEM((16, 8, 4, LANES), F32),
+            pltpu.VMEM((8, 4, LANES), F32),
+            pltpu.VMEM((8, 4, LANES), F32),
+            pltpu.SemaphoreType.DMA((48,)),
+            pltpu.SemaphoreType.DMA((48,)),
+        ],
+        compiler_params=params(16, collective_id=1, has_side_effects=True),
+    )(grad.reshape(2, 16, 8, 4, LANES))
 
 
 def on_device(sample_points, sample_spacing, crossed, colour_grad, freq, w_hidden, w_head):
-    freq4 = jnp.pad(freq[0].astype(F32), ((0, 1), (0, LANES - FREQ)))
-    halves = w_head[0].reshape(4, 2, LANES).transpose(1, 0, 2)
-    head32 = jnp.pad(halves, ((0, 0), (0, 12), (0, 0))).reshape(32, LANES)
-    picks, coords, table = sort_segments(sample_points, sample_spacing, crossed)
-    table = table.reshape(384)
-    nets, feature = gather_nets(table, coords, freq4, w_hidden[0], head32)
+    nets, feature, picks, spacing, table = gather_nets(
+        crossed.T, sample_points.transpose(1, 0, 2), sample_spacing, freq[0], w_hidden[0], w_head[0]
+    )
     nets = nets.reshape(REG, HID + 32, LANES)
-    rendered, grad = render_all(table, coords, picks, colour_grad, feature, nets)
-    parts = lax.all_to_all(grad[:, :4], "region", split_axis=0, concat_axis=0, tiled=True)
-    return rendered, jnp.sum(parts, axis=0, keepdims=True)
+    rendered, grad = render_all(table, spacing, colour_grad, picks, feature, nets)
+    return rendered, reduce_heads(grad)[None]
 
 
 def solution(mesh):

time: 117 us -> 101 us (0.86)
  blocking collectives: 21.4 us -> 0 us
  Pallas kernels: 82 us -> 90.7 us
  local copies, waits for them, and re-layouts: 10.9 us -> 9.2 us
  other arithmetic: 1.44 us -> 0 us
    all_to_all x1 -> x0, blocking collectives: 21.4 us -> none  [on_device(): lax.all_to_all(grad[:, :4], 'region', split_axis=0, concat_axis=0, tiled=...]
    pallas_call x1, Pallas kernels: 2.9 us -> 14.3 us  [reduce_heads(): pl.pallas_call(reduce_kernel, out_shape=jax.ShapeDtypeStruct((4, HID), F3...]
    pallas_call x1, Pallas kernels: 49 us -> 47.4 us  [gather_nets(): pl.pallas_call(gather_kernel, out_shape=(jax.ShapeDtypeStruct((4, 4, 4, 2...]
    slice x1 -> x0, local copies, waits for them, and re-layouts: 1.29 us -> none  [on_device(): grad[:, :4]]
    unnamed x14 -> x21, local copies, waits for them, and re-layouts: 8.89 us -> 9.2 us
where the time goes in v3:
time: 101 us
  Pallas kernels  90.7 us (90%)
  local copies, waits for them, and re-layouts  9.2 us (9%)
    pallas_call x1, Pallas kernels, gather_nets(): pl.pallas_call(gather_kernel, out_shape=(jax.ShapeDtypeStruct((4, 4, 4, 2...  47.4 us
    pallas_call x1, Pallas kernels, render_all(): pl.pallas_call(render_kernel, out_shape=(jax.ShapeDtypeStruct((3, RAYS),...  28.9 us
    pallas_call x1, Pallas kernels, reduce_heads(): pl.pallas_call(reduce_kernel, out_shape=jax.ShapeDtypeStruct((4, HID), F3...  14.3 us
    unnamed x21, local copies, waits for them, and re-layouts  9.2 us

profile of v3, /device:TPU:1, one launch (start us, length us, event | category | flops | bytes accessed | tf_op | source)
XLA Modules:
  0.0 100.6 jit_solution(14795703177262634876)
XLA Ops:
  0.6 0.0 copy-start.2
  0.6 1.0 copy-done.2
  1.6 0.0 copy-start.4
  1.6 0.9 copy-done.4
  2.5 0.0 copy-start.5
  2.5 0.8 copy-done.5
  3.4 0.0 copy-start.6
  3.4 0.7 copy-done.6
  4.1 0.0 copy-start.7
  4.1 0.7 copy-done.7
  4.7 0.0 copy-start.9
  4.7 0.7 copy-done.9
  5.4 47.4 %shard_map.86 = (bf16[4,4,4,2,288,128]{5,4,3,2,1,0:T(8,128)(2,1)}, bf16[352,128,128]{2,1,0:T(8,128)(2,1)}, bf16[4,352,1024]{2,1,0:T(8,128)(2,1)S(1)}, f32[352,128]{1,0:T(8,128)S(1)}, s32[1,384]{1,0:T(1,128)S(1)}) custom-call(s32[4,256]{1,0:T(4,128)S(1)} %bitcast.12, f32[3,256,128]{2,1,0:T(8,128)S(1)} %bitcast.9, f32[256,128]{1,0:T(8,128)S(1)} %copy-done.4, ...), custom_call_target="tpu_custom_call" | custom-call | tf_op jit(solution)/shard_map/pallas_call | solution.py:617
  52.9 0.0 copy-start
  52.9 1.6 %copy-done = bf16[4,352,1024]{2,1,0:T(8,128)(2,1)} copy-done((bf16[4,352,1024]{2,1,0:T(8,128)(2,1)}, bf16[4,352,1024]{2,1,0:T(8,128)(2,1)S(1)}, u32[]{:S(2)}) %copy-start) | copy-done | bytes 2883608
  54.5 0.0 copy-start.3
  54.5 0.7 copy-done.3
  55.1 0.0 copy-start.8
  55.1 0.6 copy-done.8
  55.7 28.9 %shard_map.87 = (f32[3,256]{1,0:T(4,128)}, f32[2,128,4,128]{3,2,1,0:T(4,128)}) custom-call(s32[1,384]{1,0:T(1,128)} %copy-done.8, f32[352,128]{1,0:T(8,128)} %copy-done.3, f32[3,256]{1,0:T(4,128)} %colour_grad_ref.1, bf16[4,352,1024]{2,1,0:T(8,128)(2,1)} %copy-done, bf16[352,128,128]{2,1,0:T(8,128)(2,1)} %get-tuple-element.12.feature_hbm_ref, ...), custom_call_target="tpu_custom_call" | custom-call | tf_op jit(solution)/shard_map/pallas_call | solution.py:654
  84.6 0.0 copy-start.1
  84.7 1.0 %copy-done.1 = f32[2,128,4,128]{3,2,1,0:T(4,128)S(1)} copy-done((f32[2,128,4,128]{3,2,1,0:T(4,128)S(1)}, f32[2,128,4,128]{3,2,1,0:T(4,128)}, u32[]{:S(2)}) %copy-start.1) | copy-done | bytes 524312
  85.7 14.3 %shard_map.88 = f32[4,256]{1,0:T(4,128)S(1)} custom-call(f32[2,16,8,4,128]{4,3,2,1,0:T(4,128)S(1)} %bitcast.8), custom_call_target="tpu_custom_call" | custom-call | tf_op jit(solution)/shard_map/pallas_call | solution.py:738
  100.0 0.6 copy.10
Async XLA Ops:
  0.6 1.0 copy-start.2
  1.6 0.9 copy-start.4
  2.5 0.8 copy-start.5
  3.4 0.7 copy-start.6
  4.1 0.7 copy-start.7
  4.7 0.7 copy-start.9
  52.9 1.6 %copy-start = (bf16[4,352,1024]{2,1,0:T(8,128)(2,1)}, bf16[4,352,1024]{2,1,0:T(8,128)(2,1)S(1)}, u32[]{:S(2)}) copy-start(bf16[4,352,1024]{2,1,0:T(8,128)(2,1)S(1)} %get-tuple-element.11.picks_hbm_ref) | copy-start | bytes 8650756
  54.5 0.7 copy-start.3
  55.1 0.6 copy-start.8
  84.6 1.0 %copy-start.1 = (f32[2,128,4,128]{3,2,1,0:T(4,128)S(1)}, f32[2,128,4,128]{3,2,1,0:T(4,128)}, u32[]{:S(2)}) copy-start(f32[2,128,4,128]{3,2,1,0:T(4,128)} %get-tuple-element.15) | copy-start | bytes 1572868

commit v4 on v3

--- a/solution.py
+++ b/solution.py
@@ -17,10 +17,16 @@
 FREQ = 64
 HID = 256
 LANES = 128
+NETS = HID + 8
+PART = NETS // 3
 COPIES = 152
 GF = 32
-CHUNKS = (4, 3, 2, 1, 1)
-GR = 16
+CHUNKS = (2, 3, 2, 1, 1, 1, 1)
+GR = 32
+GB = 32
+AHEAD = 3
+PARTS = 8
+BOUNDS = 376
 
 F32 = jnp.float32
 BF16 = jnp.bfloat16
@@ -83,9 +89,9 @@
     owner_of = jnp.minimum(owner_of, REG - 1.0)
     total = jnp.sum(blocks, axis=0, keepdims=True)
     table = jnp.where(iota((1, 384), 1) == 383, total, owner_of)
-    for part in range(3):
-        bound = ends[(part + 1) * 32 - 1:(part + 1) * 32]
-        table = jnp.where(iota((1, 384), 1) == 380 + part, bound, table)
+    for part in range(PARTS - 1):
+        last = (part + 1) * (REG // PARTS)
+        table = jnp.where(iota((1, 384), 1) == BOUNDS + part, ends[last - 1:last], table)
     return place.astype(jnp.int32), table.astype(jnp.int32)
 
 
@@ -192,9 +198,8 @@
         copy.wait()
     payload_ref[0:HID, :] = hidden_in_ref[...].astype(F32).T.astype(BF16)
     head = head_in_ref[...].astype(F32)
-    blank = jnp.zeros((12, LANES), F32)
-    head = jnp.concatenate([head[:, :LANES], blank, head[:, LANES:], blank], axis=0)
-    payload_ref[HID:HID + 32, :] = head.astype(BF16)
+    head = jnp.concatenate([head[:, :LANES], head[:, LANES:]], axis=0)
+    payload_ref[HID:NETS, :] = head.astype(BF16)
     freq_in = jnp.concatenate([freq_in_ref[...].astype(F32), jnp.zeros((3, FREQ), F32)], axis=1)
     freq_in = jnp.concatenate([freq_in, jnp.zeros((1, LANES), F32)], axis=0)
     freq_ref[me] = freq_in.astype(FREQ_TYPE)
@@ -258,9 +263,7 @@
 
     def make_stream(t):
         a, b, c = ORDERS[t]
-        rows = pl.ds(96 * t, 96)
-        near = pl.ds(96 * t, 48)
-        far = pl.ds(96 * t + 48, 48)
+        rows = pl.ds(PART * t, PART)
         base = dict(home)
         left = {axis: lax.rem(pos[axis] + 3, 4) for axis in range(3)}
         right = {axis: lax.rem(pos[axis] + 1, 4) for axis in range(3)}
@@ -274,19 +277,20 @@
 
         ids = {}
 
-        def send(name, axis, delta, where, part=rows, src=None):
+        def send(name, axis, delta, where, src=None):
             number = new_id()
-            source = view(where, core, part) if src is None else src
-            start(source, view(where, core, part), device(axis, delta), number)
+            source = view(where, core, rows) if src is None else src
+            start(source, view(where, core, rows), device(axis, delta), number)
             ids[name] = number
 
-        def wait(name, where, part=rows):
-            arrive(view(where, core, part), ids[name])
+        def wait(name, where):
+            arrive(view(where, core, rows), ids[name])
 
         def stage0():
             mine = payload_ref.at[rows, :]
             send("A+", a, 1, spec(), src=mine)
             send("A-", a, 3, spec(), src=mine)
+            send("A=", a, 2, spec(), src=mine)
             send("B+o", b, 1, spec(), src=mine)
             send("B-o", b, 3, spec(), src=mine)
             send("C+o", c, 1, spec(), src=mine)
@@ -299,22 +303,17 @@
             send("C-" + tag, c, 3, where)
 
         def stage1():
-            low, high = spec(a=left[a]), spec(a=right[a])
+            low, high, across = spec(a=left[a]), spec(a=right[a]), spec(a=opposite[a])
             wait("A+", low)
-            send("H+", a, 1, low, near)
             spread(low, "l")
             wait("A-", high)
-            send("H-", a, 3, high, far)
             spread(high, "r")
-            to_sibling(low, rows)
-            to_sibling(high, rows)
+            wait("A=", across)
+            spread(across, "d")
 
         def stage2():
-            across = spec(a=opposite[a])
-            wait("H+", across, near)
-            wait("H-", across, far)
-            spread(across, "d")
-            to_sibling(across, rows)
+            for chip in (left[a], right[a], opposite[a]):
+                to_sibling(spec(a=chip), rows)
 
         def line_arrivals(prefix, **kw):
             wait(prefix + "o", spec(**kw))
@@ -337,6 +336,8 @@
             to_sibling(high, rows)
 
         def stage4():
+            line_arrivals("C+", c=left[c])
+            send("CH+o", c, 1, spec(a=whole, c=left[c]))
             wait("BH+", spec(a=pl.ds(0, 2), b=opposite[b]))
             wait("BH-", spec(a=pl.ds(2, 2), b=opposite[b]))
             across = spec(a=whole, b=opposite[b])
@@ -345,8 +346,6 @@
             to_sibling(across, rows)
 
         def stage5():
-            line_arrivals("C+", c=left[c])
-            send("CH+o", c, 1, spec(a=whole, c=left[c]))
             line_arrivals("C-", c=right[c])
             wait("C-R", spec(a=whole, b=right[b], c=right[c]))
             send("CH-R", c, 3, spec(a=whole, b=right[b], c=right[c]))
@@ -368,13 +367,14 @@
             to_sibling(spec(a=whole, b=left[b], c=right[c]), rows)
             to_sibling(spec(a=whole, b=opposite[b], c=right[c]), rows)
 
-        def stage7():
-            for name, line in (("CH+o", pos[b]), ("CH+L", left[b]), ("CH-R", right[b]), ("CH-D", opposite[b])):
-                where = spec(a=whole, b=line, c=opposite[c])
-                wait(name, where)
-                to_sibling(where, rows)
-
-        return (stage0, stage1, stage2, stage3, stage4, stage5, stage6, stage7)
+        def stage7(name, line):
+            where = spec(a=whole, b=line, c=opposite[c])
+            wait(name, where)
+            to_sibling(where, rows)
+
+        lines = (("CH+o", pos[b]), ("CH+L", left[b]), ("CH-R", right[b]), ("CH-D", opposite[b]))
+        last = [functools.partial(stage7, name, line) for name, line in lines]
+        return [stage0, stage1, stage2, stage3, stage4, stage5, stage6] + last
 
     streams = [make_stream(t) for t in range(3)]
 
@@ -384,9 +384,9 @@
 
     stage(0)
     own = new_id()
-    start(payload_ref, view(home, core, pl.ds(0, 288)), sibling, own)
-    sibling_waits.append((view(home, 1 - core, pl.ds(0, 288)), own))
-    keep = pltpu.make_async_copy(payload_ref, view(home, core, pl.ds(0, 288)), local_sem)
+    start(payload_ref, view(home, core, pl.ds(0, NETS)), sibling, own)
+    sibling_waits.append((view(home, 1 - core, pl.ds(0, NETS)), own))
+    keep = pltpu.make_async_copy(payload_ref, view(home, core, pl.ds(0, NETS)), local_sem)
     keep.start()
 
     def features(first, count):
@@ -421,17 +421,19 @@
         picks_ref[q] = (iota((NB, SEG), 0) + q * NB == place).astype(F32).astype(BF16)
     picks_copy = pltpu.make_async_copy(picks_ref, picks_out_ref, input_sem.at[7])
     picks_copy.start()
+    stage(2)
     inputs[4].wait()
     inputs[5].wait()
     source = sort_sources([points_ref[0], points_ref[1], points_ref[2], spacing_ref[...]])
-    stage(2)
+    stage(3)
     spacing_out_ref[...] = sort_coords(picks_ref, source, coords_ref)
     table_copy.wait()
     pltpu.make_async_copy(many, many, freq_recv.at[1]).wait()
     done = 0
-    for number in range(3, 8):
-        count = CHUNKS[number - 3]
-        features(done, count)
+    for number in range(4, 11):
+        count = CHUNKS[number - 4]
+        if count:
+            features(done, count)
         done += count
         stage(number)
     for ref, number in sibling_waits:
@@ -460,60 +462,73 @@
 
 def render_kernel(
     table_ref, spacing_ref, colour_grad_ref, picks_hbm_ref, feature_hbm_ref, nets_hbm_ref,
-    rendered_ref, grad_ref, hidden_ref, raw_ref, feature_ref, nets_ref, picks_ref,
+    rendered_ref, grad_out_ref, hidden_ref, raw_ref, feature_ref, nets_ref, picks_ref, grad_ref,
     feature_sem, nets_sem, picks_sem,
 ):
     total = table_ref[0, 383]
 
+    groups = lax.div(total + (GR - 1), GR)
+
     def net_copy(part):
-        rows = pl.ds(part * 32, 32)
+        rows = pl.ds(part * (REG // PARTS), REG // PARTS)
         return pltpu.make_async_copy(nets_hbm_ref.at[rows], nets_ref.at[rows], nets_sem.at[part])
 
     def feature_copy(step):
         rows = pl.ds(step * GR, GR)
         return pltpu.make_async_copy(feature_hbm_ref.at[rows], feature_ref.at[rows], feature_sem.at[step])
 
-    for part in range(4):
-        net_copy(part).start()
-        for step in range(NB // GR):
-            if step * 4 // (NB // GR) == part:
-                feature_copy(step).start()
-
+    net_copy(0).start()
+    feature_copy(0).start()
+    net_copy(1).start()
+    for step in range(1, AHEAD):
+        feature_copy(step).start()
     picks_copy = pltpu.make_async_copy(picks_hbm_ref, picks_ref, picks_sem)
-    picks_copy.start()
-    groups = lax.div(total + (GR - 1), GR)
+
+    def raw_of(step):
+        outs = []
+        for j in range(GR):
+            b = step * GR + j
+            head = nets_ref[table_ref[0, b], HID:NETS, :].astype(F32)
+            head = jnp.concatenate([head[0:4], head[4:8]], axis=1)
+            head = jnp.concatenate([head, jnp.zeros((4, HID), F32)], axis=0).astype(BF16)
+            outs.append(dot(head, hidden_ref[b]))
+        for j in range(GR):
+            raw_ref[pl.ds((step * GR + j) * 8, 8), :] = outs[j]
 
     def forward(step, carry):
+        @pl.when(step + AHEAD < groups)
+        def _():
+            feature_copy(step + AHEAD).start()
+
         feature_copy(step).wait()
-        hids = []
+        raw_of(jnp.maximum(step - 1, 0))
         for j in range(GR):
             b = step * GR + j
             hid = dot(nets_ref[table_ref[0, b], 0:HID, :], feature_ref[b])
-            hid = jnp.maximum(hid, 0.0).astype(BF16)
-            hidden_ref[b] = hid
-            hids.append(hid)
-        for j in range(GR):
-            b = step * GR + j
-            region = table_ref[0, b]
-            head = jnp.concatenate(
-                [nets_ref[region, HID:HID + 16, :], nets_ref[region, HID + 16:HID + 32, :]], axis=1
-            )
-            raw_ref[pl.ds(b * 8, 8), :] = dot(head, hids[j])[0:8]
+            hidden_ref[b] = jnp.maximum(hid, 0.0).astype(BF16)
         return carry
 
     def blank(step, carry):
-        feature_copy(step).wait()
         for j in range(GR):
             raw_ref[pl.ds((step * GR + j) * 8, 8), :] = jnp.zeros((8, LANES), F32)
         return carry
 
     first = 0
-    for part in range(4):
+    for part in range(PARTS):
+        if part + 2 < PARTS:
+            net_copy(part + 2).start()
+        elif part + 2 == PARTS:
+            picks_copy.start()
         net_copy(part).wait()
-        last = groups if part == 3 else lax.div(table_ref[0, 380 + part], GR)
+        last = groups if part == PARTS - 1 else lax.div(table_ref[0, BOUNDS + part], GR)
         lax.fori_loop(first, last, forward, 0)
         first = last
+    raw_of(groups - 1)
     lax.fori_loop(groups, NB // GR, blank, 0)
+    for step in range(AHEAD):
+        @pl.when(step >= groups)
+        def _(step=step):
+            feature_copy(step).wait()
 
     raw = [raw_ref[pl.ds(o, NB, stride=8), :] for o in range(4)]
     spacing = spacing_ref[...]
@@ -589,18 +604,25 @@
     grad_ref[...] = jnp.zeros_like(grad_ref)
 
     def backward(step, carry):
+        total_grad, before_region = carry
         parts = []
-        for j in range(GR):
-            b = step * GR + j
+        for j in range(GB):
+            b = step * GB + j
             rg = raw_ref[pl.ds(b * 8, 8), :].astype(BF16)
             parts.append(dot(rg, hidden_ref[b], ((1,), (1,))))
-        for j in range(GR):
-            region = table_ref[0, step * GR + j]
-            grad_ref[0, region] += parts[j][0:4, :LANES]
-            grad_ref[1, region] += parts[j][0:4, LANES:]
-        return carry
-
-    lax.fori_loop(0, groups, backward, 0)
+        for j in range(GB):
+            region = table_ref[0, step * GB + j]
+            total_grad = parts[j] + jnp.where(region == before_region, total_grad, 0.0)
+            grad_ref[0, region] = total_grad[0:4, :LANES]
+            grad_ref[1, region] = total_grad[0:4, LANES:]
+            before_region = region
+        return total_grad, before_region
+
+    start = (jnp.zeros((8, HID), F32), jnp.int32(-1))
+    lax.fori_loop(0, lax.div(total + (GB - 1), GB), backward, start)
+    grad_copy = pltpu.make_async_copy(grad_ref, grad_out_ref, picks_sem)
+    grad_copy.start()
+    grad_copy.wait()
 
 
 def exact_dot_last(after):
@@ -617,16 +639,16 @@
     return pl.pallas_call(
         gather_kernel,
         out_shape=(
-            jax.ShapeDtypeStruct((4, 4, 4, 2, HID + 32, LANES), BF16),
+            jax.ShapeDtypeStruct((4, 4, 4, 2, NETS, LANES), BF16),
             jax.ShapeDtypeStruct((NB, LANES, LANES), BF16),
             jax.ShapeDtypeStruct((4, NB, SEG), BF16),
             jax.ShapeDtypeStruct((NB, LANES), F32),
             jax.ShapeDtypeStruct((1, 384), jnp.int32),
         ),
-        in_specs=[ANY] * 6,
+        in_specs=[HBM] * 6,
         out_specs=(HBM, HBM, HBM, VM, VM),
         scratch_shapes=[
-            pltpu.VMEM((HID + 32, LANES), BF16),
+            pltpu.VMEM((NETS, LANES), BF16),
             pltpu.VMEM((REG, 4, LANES), FREQ_TYPE),
             pltpu.VMEM((NB, LANES, LANES), BF16),
             pltpu.VMEM((4, NB, SEG), BF16),
@@ -646,7 +668,7 @@
             pltpu.SemaphoreType.DMA((NB // GF,)),
             pltpu.SemaphoreType.DMA((8,)),
         ],
-        compiler_params=params(50, collective_id=0, has_side_effects=True),
+        compiler_params=params(62, collective_id=0, has_side_effects=True),
     )(crossed, points, spacing, freq, hidden, head)
 
 
@@ -658,28 +680,32 @@
             jax.ShapeDtypeStruct((2, REG, 4, LANES), F32),
         ),
         in_specs=[SM, VM, VM, HBM, HBM, HBM],
-        out_specs=(VM, VM),
+        out_specs=(VM, HBM),
         scratch_shapes=[
             pltpu.VMEM((NB, HID, LANES), BF16),
             pltpu.VMEM((NB * 8, LANES), F32),
             pltpu.VMEM((NB, LANES, LANES), BF16),
-            pltpu.VMEM((REG, HID + 32, LANES), BF16),
+            pltpu.VMEM((REG, NETS, LANES), BF16),
             pltpu.VMEM((4, NB, SEG), BF16),
+            pltpu.VMEM((2, REG, 4, LANES), F32),
             pltpu.SemaphoreType.DMA((NB // GR,)),
-            pltpu.SemaphoreType.DMA((4,)),
+            pltpu.SemaphoreType.DMA((PARTS,)),
             pltpu.SemaphoreType.DMA,
         ],
-        compiler_params=params(60),
+        compiler_params=params(62),
     )(table, spacing, colour_grad, picks, feature, nets)
 
 
 def reduce_kernel(
-    grad_ref, out_ref, got_a, sum_a, last_a, got_b, sum_b, last_b, send_sem, recv_sem
+    grad_hbm_ref, out_ref, grad_ref, got_a, sum_a, last_a, got_b, sum_b, last_b, send_sem, recv_sem, load_sem
 ):
+    load = pltpu.make_async_copy(grad_hbm_ref, grad_ref, load_sem)
+    load.start()
     me = lax.axis_index("region")
     base, inner, outer = me - lax.rem(me, 8), lax.rem(me, 8), lax.div(me, 8)
     barrier = pltpu.get_barrier_semaphore()
     greet(barrier, me)
+    load.wait()
     pl.semaphore_wait(barrier, 22)
     within = lambda step: base + lax.rem(inner + step, 8)
     across = lambda step: lax.rem(outer + step, 16) * 8 + inner
@@ -738,9 +764,10 @@
     return pl.pallas_call(
         reduce_kernel,
         out_shape=jax.ShapeDtypeStruct((4, HID), F32),
-        in_specs=[VM],
+        in_specs=[HBM],
         out_specs=VM,
         scratch_shapes=[
+            pltpu.VMEM((2, 16, 8, 4, LANES), F32),
             pltpu.VMEM((8, 16, 4, LANES), F32),
             pltpu.VMEM((16, 4, LANES), F32),
             pltpu.VMEM((16, 4, LANES), F32),
@@ -749,8 +776,9 @@
             pltpu.VMEM((8, 4, LANES), F32),
             pltpu.SemaphoreType.DMA((48,)),
             pltpu.SemaphoreType.DMA((48,)),
+            pltpu.SemaphoreType.DMA,
         ],
-        compiler_params=params(16, collective_id=1, has_side_effects=True),
+        compiler_params=params(62, collective_id=1, has_side_effects=True),
     )(grad.reshape(2, 16, 8, 4, LANES))
 
 
@@ -758,7 +786,7 @@
     nets, feature, picks, spacing, table = gather_nets(
         crossed.T, sample_points.transpose(1, 0, 2), sample_spacing, freq[0], w_hidden[0], w_head[0]
     )
-    nets = nets.reshape(REG, HID + 32, LANES)
+    nets = nets.reshape(REG, NETS, LANES)
     rendered, grad = render_all(table, spacing, colour_grad, picks, feature, nets)
     return rendered, reduce_heads(grad)[None]
 

time: 101 us -> 84.2 us (0.83)
  Pallas kernels: 90.7 us -> 82 us
  local copies, waits for them, and re-layouts: 9.2 us -> 1.26 us
    unnamed x21 -> x1, local copies, waits for them, and re-layouts: 9.2 us -> 1.26 us
    pallas_call x1, Pallas kernels: 47.4 us -> 41.4 us  [gather_nets(): pl.pallas_call(gather_kernel, out_shape=(jax.ShapeDtypeStruct((4, 4, 4, 2...]
    pallas_call x1, Pallas kernels: 28.9 us -> 25.6 us  [render_all(): pl.pallas_call(render_kernel, out_shape=(jax.ShapeDtypeStruct((3, RAYS),...]
where the time goes in v4:
time: 84.2 us; the launch traced here: 84 us
  Pallas kernels  82 us (97%)
  local copies, waits for them, and re-layouts  1.26 us (1%)
    pallas_call x1, Pallas kernels, gather_nets(): pl.pallas_call(gather_kernel, out_shape=(jax.ShapeDtypeStruct((4, 4, 4, 2...  41.4 us
    pallas_call x1, Pallas kernels, render_all(): pl.pallas_call(render_kernel, out_shape=(jax.ShapeDtypeStruct((3, RAYS),...  25.6 us
    pallas_call x1, Pallas kernels, reduce_heads(): pl.pallas_call(reduce_kernel, out_shape=jax.ShapeDtypeStruct((4, HID), F3...  15 us

profile of v4, /device:TPU:1, one launch (start us, length us, event | category | flops | bytes accessed | tf_op | source)
XLA Modules:
  0.0 84.0 jit_solution(6818059826931771797)
XLA Ops:
  0.6 41.4 %shard_map.86 = (bf16[4,4,4,2,264,128]{5,4,3,2,1,0:T(8,128)(2,1)}, bf16[352,128,128]{2,1,0:T(8,128)(2,1)}, bf16[4,352,1024]{2,1,0:T(8,128)(2,1)}, f32[352,128]{1,0:T(8,128)}, s32[1,384]{1,0:T(1,128)}) custom-call(s32[4,256]{1,0:T(4,128)} %bitcast.13, f32[3,256,128]{2,1,0:T(8,128)} %bitcast.10, f32[256,128]{1,0:T(8,128)} %spacing_hbm.1, ...), custom_call_target="tpu_custom_call" | custom-call | tf_op jit(solution)/shard_map/pallas_call | solution.py:639
  42.1 25.6 %shard_map.87 = (f32[3,256]{1,0:T(4,128)}, f32[2,128,4,128]{3,2,1,0:T(4,128)}) custom-call(s32[1,384]{1,0:T(1,128)} %get-tuple-element.9.table_ref, f32[352,128]{1,0:T(8,128)} %get-tuple-element.10.spacing_ref, f32[3,256]{1,0:T(4,128)} %colour_grad_ref.1, bf16[4,352,1024]{2,1,0:T(8,128)(2,1)} %get-tuple-element.11.picks_hbm_ref, ...), custom_call_target="tpu_custom_call" | custom-call | tf_op jit(solution)/shard_map/pallas_call | solution.py:676
  67.7 15.0 %shard_map.88 = f32[4,256]{1,0:T(4,128)} custom-call(f32[2,16,8,4,128]{4,3,2,1,0:T(4,128)} %bitcast.9), custom_call_target="tpu_custom_call" | custom-call | tf_op jit(solution)/shard_map/pallas_call | solution.py:764
  82.7 1.3 %copy.10 = f32[1,4,256]{2,1,0:T(4,128)} copy(f32[1,4,256]{2,1,0:T(4,128)} %bitcast.12) | data formatting | bytes 8192

commit v5 on v4

--- a/solution.py
+++ b/solution.py
@@ -19,7 +19,7 @@
 LANES = 128
 NETS = HID + 8
 PART = NETS // 3
-COPIES = 152
+COPIES = 96
 GF = 32
 CHUNKS = (2, 3, 2, 1, 1, 1, 1)
 GR = 32
@@ -225,7 +225,6 @@
     lax.fori_loop(1, 8, freq_within, 0)
 
     counter = [0]
-    sends = []
 
     def new_id():
         counter[0] += 1
@@ -238,26 +237,21 @@
         return nets_ref.at[where[0], where[1], where[2], parity, rows, :]
 
     def start(src, dst, peer, number):
-        copy = pltpu.make_async_remote_copy(
-            src, dst, send_sem.at[number], recv_sem.at[number],
+        pltpu.make_async_remote_copy(
+            src, dst, send_sem, recv_sem.at[number],
             device_id=(peer,), device_id_type=MESH_ID,
-        )
-        copy.start()
-        sends.append(copy)
+        ).start()
 
     def arrive(dst, number):
         pltpu.make_async_remote_copy(
-            dst, dst, send_sem.at[number], recv_sem.at[number],
+            dst, dst, send_sem, recv_sem.at[number],
             device_id=(sibling,), device_id_type=MESH_ID,
         ).wait_recv()
 
     home = {0: pos[0], 1: pos[1], 2: pos[2]}
-    sibling_waits = []
 
     def to_sibling(where, rows):
-        number = new_id()
-        start(view(where, core, rows), view(where, core, rows), sibling, number)
-        sibling_waits.append((view(where, 1 - core, rows), number))
+        start(view(where, core, rows), view(where, core, rows), sibling, COPIES)
 
     whole = pl.ds(0, 4)
 
@@ -383,9 +377,7 @@
             stream[number]()
 
     stage(0)
-    own = new_id()
-    start(payload_ref, view(home, core, pl.ds(0, NETS)), sibling, own)
-    sibling_waits.append((view(home, 1 - core, pl.ds(0, NETS)), own))
+    start(payload_ref, view(home, core, pl.ds(0, NETS)), sibling, COPIES)
     keep = pltpu.make_async_copy(payload_ref, view(home, core, pl.ds(0, NETS)), local_sem)
     keep.start()
 
@@ -436,10 +428,10 @@
             features(done, count)
         done += count
         stage(number)
-    for ref, number in sibling_waits:
-        arrive(ref, number)
-    for copy in sends:
-        copy.wait_send()
+    half = nets_ref.at[pl.ds(0, 2)]
+    pltpu.make_async_copy(half, half, recv_sem.at[COPIES]).wait()
+    for sent in (half, nets_ref.at[0], nets_ref.at[0, pl.ds(0, 3)], nets_ref.at[0, 0, pl.ds(0, 3)], nets_ref.at[0, 0, 0, 0]):
+        pltpu.make_async_copy(sent, sent, send_sem).wait()
     pltpu.make_async_copy(seven, seven, freq_send.at[0]).wait()
     pltpu.make_async_copy(many, many, freq_send.at[1]).wait()
     keep.wait()
@@ -660,8 +652,8 @@
             pltpu.VMEM((3, FREQ), BF16),
             pltpu.VMEM((LANES, HID), BF16),
             pltpu.VMEM((4, HID), BF16),
-            pltpu.SemaphoreType.DMA((COPIES,)),
-            pltpu.SemaphoreType.DMA((COPIES,)),
+            pltpu.SemaphoreType.DMA,
+            pltpu.SemaphoreType.DMA((COPIES + 1,)),
             pltpu.SemaphoreType.DMA((2,)),
             pltpu.SemaphoreType.DMA((2,)),
             pltpu.SemaphoreType.DMA,
@@ -710,54 +702,49 @@
     within = lambda step: base + lax.rem(inner + step, 8)
     across = lambda step: lax.rem(outer + step, 16) * 8 + inner
 
-    def copy(src, dst, number, peer):
-        return pltpu.make_async_remote_copy(
+    def send(src, dst, number, peer):
+        pltpu.make_async_remote_copy(
             src, dst, send_sem.at[number], recv_sem.at[number],
             device_id=(peer,), device_id_type=MESH_ID,
-        )
-
-    def each(count, first, make):
-        def body(step, carry):
-            make(step, first + step)
-            return carry
-
-        lax.fori_loop(1, count, body, 0)
-
-    sent_a = lambda step: grad_ref.at[0, :, lax.rem(inner + step, 8)]
-    sent_b = lambda step: grad_ref.at[1, lax.rem(outer + step, 16)]
-    each(8, 0, lambda step, n: copy(sent_a(step), got_a.at[step], n, within(step)).start())
-    each(16, 8, lambda step, n: copy(sent_b(step), got_b.at[step], n, across(step)).start())
-
-    def add_a(step, total):
-        copy(sent_a(step), got_a.at[step], step, within(step)).wait_recv()
-        return total + got_a[step]
-
-    sum_a[...] = lax.fori_loop(1, 8, add_a, grad_ref[0, :, inner])
-    part_a = lambda step: sum_a.at[lax.rem(outer + step, 16)]
-    each(16, 24, lambda step, n: copy(part_a(step), last_a.at[step], n, across(step)).start())
-
-    def add_b(step, total):
-        copy(sent_b(step), got_b.at[step], 8 + step, across(step)).wait_recv()
-        return total + got_b[step]
-
-    sum_b[...] = lax.fori_loop(1, 16, add_b, grad_ref[1, outer])
-    part_b = lambda step: sum_b.at[lax.rem(inner + step, 8)]
-    each(8, 40, lambda step, n: copy(part_b(step), last_b.at[step], n, within(step)).start())
-
-    def end_a(step, total):
-        copy(part_a(step), last_a.at[step], 24 + step, across(step)).wait_recv()
-        return total + last_a[step]
-
-    def end_b(step, total):
-        copy(part_b(step), last_b.at[step], 40 + step, within(step)).wait_recv()
-        return total + last_b[step]
-
-    out_ref[:, :LANES] = lax.fori_loop(1, 16, end_a, sum_a[outer])
-    out_ref[:, LANES:] = lax.fori_loop(1, 8, end_b, sum_b[inner])
-    each(8, 0, lambda step, n: copy(sent_a(step), got_a.at[step], n, within(step)).wait_send())
-    each(16, 8, lambda step, n: copy(sent_b(step), got_b.at[step], n, across(step)).wait_send())
-    each(16, 24, lambda step, n: copy(part_a(step), last_a.at[step], n, across(step)).wait_send())
-    each(8, 40, lambda step, n: copy(part_b(step), last_b.at[step], n, within(step)).wait_send())
+        ).start()
+
+    def finish(ref, sem):
+        pltpu.make_async_copy(ref, ref, sem).wait()
+
+    rest_a, rest_b = got_a.at[pl.ds(1, 7)], got_b.at[pl.ds(1, 15)]
+    end_a, end_b = last_a.at[pl.ds(1, 15)], last_b.at[pl.ds(1, 7)]
+    for step in range(1, 16):
+        send(grad_ref.at[1, lax.rem(outer + step, 16)], got_b.at[step], 0, across(step))
+    for step in range(1, 8):
+        send(grad_ref.at[0, :, lax.rem(inner + step, 8)], got_a.at[step], 1, within(step))
+    finish(rest_b, recv_sem.at[0])
+    total = grad_ref[1, outer]
+    for step in range(1, 16):
+        total = total + got_b[step]
+    sum_b[...] = total
+    for step in range(1, 8):
+        send(sum_b.at[lax.rem(inner + step, 8)], last_b.at[step], 2, within(step))
+    finish(rest_a, recv_sem.at[1])
+    total = grad_ref[0, :, inner]
+    for step in range(1, 8):
+        total = total + got_a[step]
+    sum_a[...] = total
+    for step in range(1, 16):
+        send(sum_a.at[lax.rem(outer + step, 16)], last_a.at[step], 3, across(step))
+    finish(end_b, recv_sem.at[2])
+    total = sum_b[inner]
+    for step in range(1, 8):
+        total = total + last_b[step]
+    out_ref[:, LANES:] = total
+    finish(end_a, recv_sem.at[3])
+    total = sum_a[outer]
+    for step in range(1, 16):
+        total = total + last_a[step]
+    out_ref[:, :LANES] = total
+    finish(rest_b, send_sem.at[0])
+    finish(rest_a, send_sem.at[1])
+    finish(end_b, send_sem.at[2])
+    finish(end_a, send_sem.at[3])
 
 
 def reduce_heads(grad):
@@ -774,8 +761,8 @@
             pltpu.VMEM((16, 8, 4, LANES), F32),
             pltpu.VMEM((8, 4, LANES), F32),
             pltpu.VMEM((8, 4, LANES), F32),
-            pltpu.SemaphoreType.DMA((48,)),
-            pltpu.SemaphoreType.DMA((48,)),
+            pltpu.SemaphoreType.DMA((4,)),
+            pltpu.SemaphoreType.DMA((4,)),
             pltpu.SemaphoreType.DMA,
         ],
         compiler_params=params(62, collective_id=1, has_side_effects=True),

time: 84.2 us -> 81.6 us (0.969)
  Pallas kernels: 82 us -> 79.1 us
    pallas_call x1, Pallas kernels: 41.4 us -> 39.4 us  [gather_nets(): pl.pallas_call(gather_kernel, out_shape=(jax.ShapeDtypeStruct((4, 4, 4, 2...]
    pallas_call x1, Pallas kernels: 15 us -> 13.8 us  [reduce_heads(): pl.pallas_call(reduce_kernel, out_shape=jax.ShapeDtypeStruct((4, HID), F3...]
where the time goes in v5:
time: 81.6 us; the launch traced here: 81 us
  Pallas kernels  79.1 us (97%)
  local copies, waits for them, and re-layouts  1.26 us (2%)
    pallas_call x1, Pallas kernels, gather_nets(): pl.pallas_call(gather_kernel, out_shape=(jax.ShapeDtypeStruct((4, 4, 4, 2...  39.4 us
    pallas_call x1, Pallas kernels, render_all(): pl.pallas_call(render_kernel, out_shape=(jax.ShapeDtypeStruct((3, RAYS),...  25.9 us
    pallas_call x1, Pallas kernels, reduce_heads(): pl.pallas_call(reduce_kernel, out_shape=jax.ShapeDtypeStruct((4, HID), F3...  13.8 us

profile of v5, /device:TPU:1, one launch (start us, length us, event | category | flops | bytes accessed | tf_op | source)
XLA Modules:
  0.0 81.0 jit_solution(7391768462236196781)
XLA Ops:
  0.6 39.4 %shard_map.86 = (bf16[4,4,4,2,264,128]{5,4,3,2,1,0:T(8,128)(2,1)}, bf16[352,128,128]{2,1,0:T(8,128)(2,1)}, bf16[4,352,1024]{2,1,0:T(8,128)(2,1)}, f32[352,128]{1,0:T(8,128)}, s32[1,384]{1,0:T(1,128)}) custom-call(s32[4,256]{1,0:T(4,128)} %bitcast.13, f32[3,256,128]{2,1,0:T(8,128)} %bitcast.10, f32[256,128]{1,0:T(8,128)} %spacing_hbm.1, ...), custom_call_target="tpu_custom_call" | custom-call | tf_op jit(solution)/shard_map/pallas_call | solution.py:631
  40.0 25.9 %shard_map.87 = (f32[3,256]{1,0:T(4,128)}, f32[2,128,4,128]{3,2,1,0:T(4,128)}) custom-call(s32[1,384]{1,0:T(1,128)} %get-tuple-element.9.table_ref, f32[352,128]{1,0:T(8,128)} %get-tuple-element.10.spacing_ref, f32[3,256]{1,0:T(4,128)} %colour_grad_ref.1, bf16[4,352,1024]{2,1,0:T(8,128)(2,1)} %get-tuple-element.11.picks_hbm_ref, ...), custom_call_target="tpu_custom_call" | custom-call | tf_op jit(solution)/shard_map/pallas_call | solution.py:668
  66.0 13.8 %shard_map.88 = f32[4,256]{1,0:T(4,128)} custom-call(f32[2,16,8,4,128]{4,3,2,1,0:T(4,128)} %bitcast.9), custom_call_target="tpu_custom_call" | custom-call | tf_op jit(solution)/shard_map/pallas_call | solution.py:751
  79.7 1.3 %copy.10 = f32[1,4,256]{2,1,0:T(4,128)} copy(f32[1,4,256]{2,1,0:T(4,128)} %bitcast.12) | data formatting | bytes 8192

commit v6 on v5

--- a/solution.py
+++ b/solution.py
@@ -22,9 +22,9 @@
 COPIES = 96
 GF = 32
 CHUNKS = (2, 3, 2, 1, 1, 1, 1)
-GR = 32
-GB = 32
-AHEAD = 3
+GR = 44
+GB = 44
+AHEAD = 2
 PARTS = 8
 BOUNDS = 376
 
@@ -529,7 +529,8 @@
     colour = [1.0 / (1.0 + jnp.exp(-raw[c])) for c in (1, 2, 3)]
     gate = 1.0 / (1.0 + jnp.exp(-raw[0]))
     optical = soft * spacing
-    running = exact_dot(optical, tri("upto"))
+    sums = exact_dot(optical, jnp.concatenate([tri("upto"), tri("all")], axis=1))
+    running, passed = sums[:, :LANES], jnp.exp(-sums[:, LANES:])
     after = jnp.exp(-running)
     weight = jnp.exp(optical - running) * (1.0 - jnp.exp(-optical))
     chooser = (iota((8, LANES), 1) // S == iota((8, LANES), 0)).astype(F32).astype(BF16)
@@ -574,17 +575,18 @@
     hi, mid, low = pieces(grad_rows)
     grad_rows = jnp.concatenate(
         [hi.astype(F32), mid.astype(F32), low.astype(F32), jnp.zeros((4, SEG), F32)], axis=0
-    ).astype(BF16)
-    spread = [jnp.zeros((NB, LANES), F32) for _ in range(4)]
+    )
+    got = jnp.zeros((NB, 64), F32)
     for q in range(4):
-        got = dot(picks_ref[q], grad_rows, ((1,), (1,))).astype(BF16)
-        lane = iota((16, LANES), 1) // S == q
-        for o in range(4):
-            row = iota((16, LANES), 0)
-            expand = (lane & (row % 4 == o) & (row < 12)).astype(F32).astype(BF16)
-            spread[o] = spread[o] + dot(got, expand)
+        parts = [grad_rows if q == other else jnp.zeros((16, SEG), F32) for other in range(4)]
+        rows = jnp.concatenate(parts, axis=0).astype(BF16)
+        got = got + dot(picks_ref[q], rows, ((1,), (1,)))
+    row, col = iota((64, 4 * LANES), 0), iota((64, 4 * LANES), 1)
+    expand = (row // 16 == col % LANES // S) & (row % 4 == col // LANES) & (row % 16 < 12)
+    wide = dot(got.astype(BF16), expand.astype(F32).astype(BF16))
+    spread = [wide[:, o * LANES:(o + 1) * LANES] for o in range(4)]
     shade = spread[0] * colour[0] + spread[1] * colour[1] + spread[2] * colour[2]
-    later = exact_dot(shade * weight, tri("after")) + spread[3] * exact_dot_last(after)
+    later = exact_dot(shade * weight, tri("after")) + spread[3] * passed
     d_optical = shade * after - later
     raw_grads = [d_optical * spacing * gate]
     for c in range(3):
@@ -615,12 +617,6 @@
     grad_copy = pltpu.make_async_copy(grad_ref, grad_out_ref, picks_sem)
     grad_copy.start()
     grad_copy.wait()
-
-
-def exact_dot_last(after):
-    row, col = iota((LANES, LANES), 0), iota((LANES, LANES), 1)
-    pattern = ((row // S == col // S) & (row % S == S - 1)).astype(F32).astype(BF16)
-    return exact_dot(after, pattern)
 
 
 def params(mib, **kw):
@@ -689,7 +685,7 @@
 
 
 def reduce_kernel(
-    grad_hbm_ref, out_ref, grad_ref, got_a, sum_a, last_a, got_b, sum_b, last_b, send_sem, recv_sem, load_sem
+    grad_hbm_ref, low_ref, high_ref, grad_ref, got_a, sum_a, last_a, got_b, sum_b, last_b, send_sem, recv_sem, load_sem
 ):
     load = pltpu.make_async_copy(grad_hbm_ref, grad_ref, load_sem)
     load.start()
@@ -735,12 +731,12 @@
     total = sum_b[inner]
     for step in range(1, 8):
         total = total + last_b[step]
-    out_ref[:, LANES:] = total
+    high_ref[...] = total
     finish(end_a, recv_sem.at[3])
     total = sum_a[outer]
     for step in range(1, 16):
         total = total + last_a[step]
-    out_ref[:, :LANES] = total
+    low_ref[...] = total
     finish(rest_b, send_sem.at[0])
     finish(rest_a, send_sem.at[1])
     finish(end_b, send_sem.at[2])
@@ -750,9 +746,9 @@
 def reduce_heads(grad):
     return pl.pallas_call(
         reduce_kernel,
-        out_shape=jax.ShapeDtypeStruct((4, HID), F32),
+        out_shape=(jax.ShapeDtypeStruct((4, LANES), F32), jax.ShapeDtypeStruct((4, LANES), F32)),
         in_specs=[HBM],
-        out_specs=VM,
+        out_specs=(VM, VM),
         scratch_shapes=[
             pltpu.VMEM((2, 16, 8, 4, LANES), F32),
             pltpu.VMEM((8, 16, 4, LANES), F32),
@@ -775,7 +771,8 @@
     )
     nets = nets.reshape(REG, NETS, LANES)
     rendered, grad = render_all(table, spacing, colour_grad, picks, feature, nets)
-    return rendered, reduce_heads(grad)[None]
+    low, high = reduce_heads(grad)
+    return rendered, jnp.concatenate([low, high], axis=1)[None]
 
 
 def solution(mesh):

time: 81.6 us -> 81.1 us (level)
  other arithmetic: 0 us -> 1.27 us
  local copies, waits for them, and re-layouts: 1.26 us -> 0 us
    broadcast_in_dim x0 -> x1, other arithmetic: none -> 1.27 us  [on_device(): return (rendered, jnp.concatenate([low, high], axis=1)[None])]
    unnamed x1 -> x0, local copies, waits for them, and re-layouts: 1.26 us -> none
where the time goes in v6:
time: 81.1 us; the launch traced here: 80.9 us
  Pallas kernels  79 us (97%)
  other arithmetic  1.27 us (2%)
    pallas_call x1, Pallas kernels, gather_nets(): pl.pallas_call(gather_kernel, out_shape=(jax.ShapeDtypeStruct((4, 4, 4, 2...  39.4 us
    pallas_call x1, Pallas kernels, render_all(): pl.pallas_call(render_kernel, out_shape=(jax.ShapeDtypeStruct((3, RAYS),...  26.3 us
    pallas_call x1, Pallas kernels, reduce_heads(): pl.pallas_call(reduce_kernel, out_shape=(jax.ShapeDtypeStruct((4, LANES),...  13.3 us

profile of v6, /device:TPU:1, one launch (start us, length us, event | category | flops | bytes accessed | tf_op | source)
XLA Modules:
  0.0 80.9 jit_solution(10096350940294135115)
XLA Ops:
  0.6 39.4 %shard_map.86 = (bf16[4,4,4,2,264,128]{5,4,3,2,1,0:T(8,128)(2,1)}, bf16[352,128,128]{2,1,0:T(8,128)(2,1)}, bf16[4,352,1024]{2,1,0:T(8,128)(2,1)}, f32[352,128]{1,0:T(8,128)}, s32[1,384]{1,0:T(1,128)}) custom-call(s32[4,256]{1,0:T(4,128)} %bitcast.13, f32[3,256,128]{2,1,0:T(8,128)} %bitcast.11, f32[256,128]{1,0:T(8,128)} %spacing_hbm.1, ...), custom_call_target="tpu_custom_call" | custom-call | tf_op jit(solution)/shard_map/pallas_call | solution.py:627
  40.0 26.3 %shard_map.87 = (f32[3,256]{1,0:T(4,128)}, f32[2,128,4,128]{3,2,1,0:T(4,128)}) custom-call(s32[1,384]{1,0:T(1,128)} %get-tuple-element.11.table_ref, f32[352,128]{1,0:T(8,128)} %get-tuple-element.12.spacing_ref, f32[3,256]{1,0:T(4,128)} %colour_grad_ref.1, bf16[4,352,1024]{2,1,0:T(8,128)(2,1)} %get-tuple-element.13.picks_hbm_ref, ...), custom_call_target="tpu_custom_call" | custom-call | tf_op jit(solution)/shard_map/pallas_call | solution.py:664
  66.3 13.3 %shard_map.88 = (f32[4,128]{1,0:T(4,128)}, f32[4,128]{1,0:T(4,128)}) custom-call(f32[2,16,8,4,128]{4,3,2,1,0:T(4,128)} %bitcast.10), custom_call_target="tpu_custom_call" | custom-call | tf_op jit(solution)/shard_map/pallas_call | solution.py:747
  79.6 1.3 %maximum_bitcast_fusion = f32[1,4,256]{2,1,0:T(4,128)} fusion(f32[4,128]{1,0:T(4,128)} %get-tuple-element.19, f32[4,128]{1,0:T(4,128)} %get-tuple-element.18), kind=kLoop, calls=%fused_computation | loop fusion | flops 1024 | bytes 8192 | tf_op jit(solution)/shard_map/broadcast_in_dim | solution.py:775

commit v7 on v6

--- a/solution.py
+++ b/solution.py
@@ -21,7 +21,7 @@
 PART = NETS // 3
 COPIES = 96
 GF = 32
-CHUNKS = (2, 3, 2, 1, 1, 1, 1)
+CHUNKS = (3, 4, 2, 1, 1, 0, 0)
 GR = 44
 GB = 44
 AHEAD = 2
@@ -222,8 +222,6 @@
         ).start()
         return carry
 
-    lax.fori_loop(1, 8, freq_within, 0)
-
     counter = [0]
 
     def new_id():
@@ -377,6 +375,7 @@
             stream[number]()
 
     stage(0)
+    lax.fori_loop(1, 8, freq_within, 0)
     start(payload_ref, view(home, core, pl.ds(0, NETS)), sibling, COPIES)
     keep = pltpu.make_async_copy(payload_ref, view(home, core, pl.ds(0, NETS)), local_sem)
     keep.start()
@@ -406,9 +405,9 @@
     table_copy = pltpu.make_async_copy(table_out_ref, table_ref, input_sem.at[6])
     table_copy.start()
     seven, many = freq_ref.at[pl.ds(0, 7)], freq_ref.at[pl.ds(0, 120)]
+    stage(1)
     pltpu.make_async_copy(seven, seven, freq_recv.at[0]).wait()
     lax.fori_loop(1, 16, freq_across, 0)
-    stage(1)
     for q in range(4):
         picks_ref[q] = (iota((NB, SEG), 0) + q * NB == place).astype(F32).astype(BF16)
     picks_copy = pltpu.make_async_copy(picks_ref, picks_out_ref, input_sem.at[7])
@@ -709,10 +708,17 @@
 
     rest_a, rest_b = got_a.at[pl.ds(1, 7)], got_b.at[pl.ds(1, 15)]
     end_a, end_b = last_a.at[pl.ds(1, 15)], last_b.at[pl.ds(1, 7)]
+    for step in range(1, 8):
+        send(grad_ref.at[0, :, lax.rem(inner + step, 8)], got_a.at[step], 1, within(step))
     for step in range(1, 16):
         send(grad_ref.at[1, lax.rem(outer + step, 16)], got_b.at[step], 0, across(step))
+    finish(rest_a, recv_sem.at[1])
+    total = grad_ref[0, :, inner]
     for step in range(1, 8):
-        send(grad_ref.at[0, :, lax.rem(inner + step, 8)], got_a.at[step], 1, within(step))
+        total = total + got_a[step]
+    sum_a[...] = total
+    for step in range(1, 16):
+        send(sum_a.at[lax.rem(outer + step, 16)], last_a.at[step], 3, across(step))
     finish(rest_b, recv_sem.at[0])
     total = grad_ref[1, outer]
     for step in range(1, 16):
@@ -720,13 +726,6 @@
     sum_b[...] = total
     for step in range(1, 8):
         send(sum_b.at[lax.rem(inner + step, 8)], last_b.at[step], 2, within(step))
-    finish(rest_a, recv_sem.at[1])
-    total = grad_ref[0, :, inner]
-    for step in range(1, 8):
-        total = total + got_a[step]
-    sum_a[...] = total
-    for step in range(1, 16):
-        send(sum_a.at[lax.rem(outer + step, 16)], last_a.at[step], 3, across(step))
     finish(end_b, recv_sem.at[2])
     total = sum_b[inner]
     for step in range(1, 8):

time: 81.1 us -> 80.4 us (level)
  Pallas kernels: 79 us -> 77.7 us
    pallas_call x1, Pallas kernels: 26.3 us -> 24.2 us  [render_all(): pl.pallas_call(render_kernel, out_shape=(jax.ShapeDtypeStruct((3, RAYS),...]
    pallas_call x1, Pallas kernels: 13.3 us -> 15.4 us  [reduce_heads(): pl.pallas_call(reduce_kernel, out_shape=(jax.ShapeDtypeStruct((4, LANES),...]
    pallas_call x1, Pallas kernels: 39.4 us -> 38.1 us  [gather_nets(): pl.pallas_call(gather_kernel, out_shape=(jax.ShapeDtypeStruct((4, 4, 4, 2...]
where the time goes in v7:
time: 80.4 us; the launch traced here: 79.6 us
  Pallas kernels  77.7 us (97%)
  other arithmetic  1.27 us (2%)
    pallas_call x1, Pallas kernels, gather_nets(): pl.pallas_call(gather_kernel, out_shape=(jax.ShapeDtypeStruct((4, 4, 4, 2...  38.1 us
    pallas_call x1, Pallas kernels, render_all(): pl.pallas_call(render_kernel, out_shape=(jax.ShapeDtypeStruct((3, RAYS),...  24.2 us
    pallas_call x1, Pallas kernels, reduce_heads(): pl.pallas_call(reduce_kernel, out_shape=(jax.ShapeDtypeStruct((4, LANES),...  15.4 us

profile of v7, /device:TPU:1, one launch (start us, length us, event | category | flops | bytes accessed | tf_op | source)
XLA Modules:
  0.0 79.6 jit_solution(8741852139975991840)
XLA Ops:
  0.6 38.1 %shard_map.86 = (bf16[4,4,4,2,264,128]{5,4,3,2,1,0:T(8,128)(2,1)}, bf16[352,128,128]{2,1,0:T(8,128)(2,1)}, bf16[4,352,1024]{2,1,0:T(8,128)(2,1)}, f32[352,128]{1,0:T(8,128)}, s32[1,384]{1,0:T(1,128)}) custom-call(s32[4,256]{1,0:T(4,128)} %bitcast.13, f32[3,256,128]{2,1,0:T(8,128)} %bitcast.11, f32[256,128]{1,0:T(8,128)} %spacing_hbm.1, ...), custom_call_target="tpu_custom_call" | custom-call | tf_op jit(solution)/shard_map/pallas_call | solution.py:626
  38.7 24.2 %shard_map.87 = (f32[3,256]{1,0:T(4,128)}, f32[2,128,4,128]{3,2,1,0:T(4,128)}) custom-call(s32[1,384]{1,0:T(1,128)} %get-tuple-element.11.table_ref, f32[352,128]{1,0:T(8,128)} %get-tuple-element.12.spacing_ref, f32[3,256]{1,0:T(4,128)} %colour_grad_ref.1, bf16[4,352,1024]{2,1,0:T(8,128)(2,1)} %get-tuple-element.13.picks_hbm_ref, ...), custom_call_target="tpu_custom_call" | custom-call | tf_op jit(solution)/shard_map/pallas_call | solution.py:663
  63.0 15.4 %shard_map.88 = (f32[4,128]{1,0:T(4,128)}, f32[4,128]{1,0:T(4,128)}) custom-call(f32[2,16,8,4,128]{4,3,2,1,0:T(4,128)} %bitcast.10), custom_call_target="tpu_custom_call" | custom-call | tf_op jit(solution)/shard_map/pallas_call | solution.py:746
  78.4 1.3 %maximum_bitcast_fusion = f32[1,4,256]{2,1,0:T(4,128)} fusion(f32[4,128]{1,0:T(4,128)} %get-tuple-element.19, f32[4,128]{1,0:T(4,128)} %get-tuple-element.18), kind=kLoop, calls=%fused_computation | loop fusion | flops 1024 | bytes 8192 | tf_op jit(solution)/shard_map/broadcast_in_dim | solution.py:774
